TPU v7x, 256 devices: a whole 4x4x8 slice. The times are simulated.
256 devices in a mesh: row: 16 (over y, z_lo), col: 16 (over x, z_hi, core).
Axes of the slice: x: 4, y: 4, z: 8 (z_hi: 2, z_lo: 4; z = z_hi * 4 + z_lo), core: 2. Of those that a mesh axis runs over, the one named last changes fastest.
Arguments:
- features: float32 [65536, 128], P(('col', 'row')), may hold values from -6 to 6
- weight: float32 [128, 128], replicated, may hold values from -4 to 4
- bias_vector: float32 [128], replicated, may hold values from -4 to 4
- out_grad: float32 [65536, 128], P(('row', 'col')), may hold values from -6 to 6
- adj_tiles: int32 [16, 16, 128, 128, 128], P('row', 'col'), may hold values 0 or 1
- tile_slots: int32 [16, 16, 128], P('row', 'col'), may hold values from 0 to 1023, as said below
- tile_counts: int32 [16, 16], P('row', 'col'), may hold values from 17 to 128, as said below
Outputs:
- activated: float32 [65536, 128], P(('row', 'col'))
- feature_grad: float32 [65536, 128], P(('col', 'row'))
- weight_grad: float32 [128, 128], replicated
- bias_grad: float32 [128], replicated
Inputs may be any that keep to these rules, and one draw needn't show every extreme that they name: `tile_slots`: each block's slots name distinct positions r * 32 + c of its 32 x 32 tiles. Some block is full in every draw; slots from tile_counts on are ignored.
All inputs are finite; a program needn't handle non-finite values. No bound on the sum of `adj_tiles` on one device may be relied on, other than what follows from the above.
Results may differ from a plain program's by a relative error of at most 0.0003.
Values sent between devices are 32-bit elements; how exact they have to be, the bound alone decides.
A program may use at most 128 MiB of HBM per device.

v0:
```python
import jax
import jax.numpy as jnp
from jax import lax
from jax.sharding import PartitionSpec as P

TILE = 128


def dense_step(aggregated, weight, bias_vector, cotangent):
    preact = jnp.dot(aggregated, weight, precision=lax.Precision.HIGHEST) + bias_vector
    logistic = jax.nn.sigmoid(preact)
    activated = preact * logistic
    pre_grad = cotangent * logistic * (1.0 + preact * (1.0 - logistic))
    weight_part = jnp.dot(aggregated.T, pre_grad, precision=lax.Precision.HIGHEST)
    bias_part = jnp.sum(pre_grad, axis=0)
    back_rows = jnp.dot(pre_grad, weight.T, precision=lax.Precision.HIGHEST)
    return (activated, weight_part, bias_part, back_rows)


def local(features, weight, bias_vector, out_grad, adj_tiles, tile_slots, tile_counts):
    row_count = lax.axis_size("row")
    col_count = lax.axis_size("col")
    node_rows = features.shape[0]
    width = features.shape[1]
    tile_rows = node_rows * col_count // TILE
    tile_cols = node_rows * row_count // TILE
    adjacency = adj_tiles[0, 0].astype(jnp.float32)
    slots = tile_slots[0, 0]
    slot_total = slots.shape[0]
    live_mask = (jnp.arange(slot_total) < tile_counts[0, 0]).astype(jnp.float32)
    tile_row = slots // tile_cols
    tile_col = slots % tile_cols
    row_select = (tile_row[:, None] == jnp.arange(tile_rows)[None, :]).astype(
        jnp.float32
    ) * live_mask[:, None]
    col_select = (tile_col[:, None] == jnp.arange(tile_cols)[None, :]).astype(
        jnp.float32
    ) * live_mask[:, None]
    dst_partial = jnp.dot(
        row_select.T, jnp.sum(adjacency, axis=2), precision=lax.Precision.HIGHEST
    ).reshape(-1)
    src_partial = jnp.dot(
        col_select.T, jnp.sum(adjacency, axis=1), precision=lax.Precision.HIGHEST
    ).reshape(-1)
    src_scale = lax.rsqrt(
        1.0 + lax.psum_scatter(src_partial, "row", scatter_dimension=0, tiled=True)
    )
    scaled = features * src_scale[:, None]
    gathered = lax.all_gather(scaled, "row", axis=0, tiled=True)
    taken = jnp.take(gathered.reshape(tile_cols, TILE, width), tile_col, axis=0)
    product = jnp.einsum(
        "kab,kbh->kah",
        adjacency,
        taken,
        precision=lax.Precision.HIGHEST,
        preferred_element_type=jnp.float32,
    )
    partial_value = jnp.einsum(
        "kr,kah->rah",
        row_select,
        product,
        precision=lax.Precision.HIGHEST,
        preferred_element_type=jnp.float32,
    ).reshape(tile_rows * TILE, width)
    dst_scale = lax.rsqrt(
        1.0 + lax.psum_scatter(dst_partial, "col", scatter_dimension=0, tiled=True)
    )
    aggregated = (
        lax.psum_scatter(partial_value, "col", scatter_dimension=0, tiled=True) * dst_scale[:, None]
    )
    activated, weight_part, bias_part, back_rows = dense_step(
        aggregated, weight, bias_vector, out_grad
    )
    weight_grad, bias_grad = lax.psum((weight_part, bias_part), ("row", "col"))
    row_grads = lax.all_gather(back_rows * dst_scale[:, None], "col", axis=0, tiled=True)
    taken_back = jnp.take(row_grads.reshape(tile_rows, TILE, width), tile_row, axis=0)
    product_back = jnp.einsum(
        "kab,kah->kbh",
        adjacency,
        taken_back,
        precision=lax.Precision.HIGHEST,
        preferred_element_type=jnp.float32,
    )
    partial_back = jnp.einsum(
        "kc,kbh->cbh",
        col_select,
        product_back,
        precision=lax.Precision.HIGHEST,
        preferred_element_type=jnp.float32,
    ).reshape(tile_cols * TILE, width)
    feature_grad = (
        lax.psum_scatter(partial_back, "row", scatter_dimension=0, tiled=True) * src_scale[:, None]
    )
    return (activated, feature_grad, weight_grad, bias_grad)


def solution(mesh):
    return jax.shard_map(
        local,
        mesh=mesh,
        in_specs=(
            P(("col", "row"), None),
            P(),
            P(),
            P(("row", "col"), None),
            P("row", "col", None, None, None),
            P("row", "col", None),
            P("row", "col"),
        ),
        out_specs=(P(("row", "col"), None), P(("col", "row"), None), P(), P()),
        check_vma=False,
    )
```

profile of v0, /device:TPU:1, one launch (start us, length us, event | category | flops | bytes accessed | tf_op | source)
XLA Modules:
  0.0 764.2 jit_solution(688655162839533169)
XLA Ops:
  7.2 0.0 copy-start
  7.2 0.0 copy-start.3
  7.2 0.0 copy-start.1
  7.2 0.0 all-gather.3.cloned.1.call-start
  7.9 1.3 dynamic-slice
  9.9 5.7 convert_reduce_fusion
  15.6 0.0 copy-done.3
  15.6 0.2 convolution_bitcast_fusion.1
  15.8 68.3 %all-reduce = f32[4096]{0:T(1024)S(1)} all-reduce(f32[4096]{0:T(1024)S(1)} %convolution_bitcast_fusion.1), channel_id=2, replica_groups=mesh['row'=16,'col'=16] {'row'}, use_global_device_ids=true, to_apply=%region_1.2.clone | all-reduce | flops 4096 | bytes 32768
  84.1 0.1 fusion.45
  84.2 0.0 copy-done.1
  84.2 0.8 broadcast_multiply_fusion.1
  85.0 0.0 all-gather.3.cloned.1.call-update
  85.0 0.0 reduce-scatter.3.cloned.1.call-start
  85.1 89.2 %all-gather.3.cloned.1.call-done = f32[4096,128]{1,0:T(8,128)} async-done(((f32[256,128]{1,0:T(8,128)}), f32[4096,128]{1,0:T(8,128)}) %all-gather.3.cloned.1.call-update) | async-done | bytes 2097168 | tf_op jit(solution)/shard_map/all_gather | solution.py:49
  174.3 5.9 gather_fusion
  180.1 21.5 %fusion.12 = f32[128,128,128]{1,2,0:T(8,128)} fusion(s32[1,1,128,128,128]{4,3,2,1,0:T(8,128)} %param.13, f32[128,128,128]{2,1,0:T(8,128)} %gather_fusion, pred[128]{0:T(512)(128)(4,1)S(1)} %get-tuple-element.14), kind=kOutput, calls=%fused_computation.16 | convolution fusion | flops 3225419776 | bytes 25165952 | tf_op jit(solution)/shard_map/kab,kbh->kah/dot_general | solution.py:51
  201.7 9.3 %copy.18 = f32[128,128,128]{2,0,1:T(8,128)} copy(f32[128,128,128]{1,2,0:T(8,128)} %fusion.12) | data formatting | bytes 16777216 | tf_op jit(solution)/shard_map/kab,kbh->kah/dot_general | solution.py:51
  211.0 0.0 copy-start.6
  211.0 0.0 copy-start.4
  211.0 0.0 copy-start.5
  211.0 6.8 fusion.30
  217.7 2.6 copy.19
  220.3 0.0 reduce-scatter.3.cloned.1.call-update
  220.3 0.0 all-gather.5.cloned.1.call-start
  220.4 0.0 copy-done.6
  220.4 0.6 dynamic-slice.2
  221.6 0.2 convolution_bitcast_fusion
  221.8 87.6 %all-reduce.1 = f32[4096]{0:T(1024)S(1)} all-reduce(f32[4096]{0:T(1024)S(1)} %convolution_bitcast_fusion), channel_id=4, replica_groups=mesh['row'=16,'col'=16] {'col'}, use_global_device_ids=true, to_apply=%region_4.6.clone | all-reduce | flops 4096 | bytes 32768
  309.4 0.1 fusion.44
  309.5 4.8 reduce-scatter.3.cloned.1.call-done
  314.3 0.0 copy-done
  314.3 0.0 copy-done.4
  314.3 0.0 copy-done.5
  314.3 1.9 fusion.52
  316.2 0.9 convolution_multiply_fusion
  317.1 0.0 all-gather.5.cloned.1.call-update
  317.2 0.0 reduce-scatter.5.cloned.1.call-start
  317.2 62.5 %all-gather.5.cloned.1.call-done = f32[4096,128]{1,0:T(8,128)} async-done(((f32[256,128]{1,0:T(8,128)}), f32[4096,128]{1,0:T(8,128)}) %all-gather.5.cloned.1.call-update) | async-done | bytes 2097168 | tf_op jit(solution)/shard_map/all_gather | solution.py:75
  379.7 5.9 gather_fusion.1
  385.6 19.7 %fusion.17 = f32[128,128,128]{1,2,0:T(8,128)} fusion(s32[1,1,128,128,128]{4,3,2,1,0:T(8,128)} %param.13, f32[128,128,128]{2,1,0:T(8,128)} %gather_fusion.1, pred[128]{0:T(512)(128)(4,1)S(1)} %get-tuple-element.9), kind=kOutput, calls=%fused_computation.17 | convolution fusion | flops 3225419776 | bytes 25165952 | tf_op jit(solution)/shard_map/kab,kah->kbh/dot_general | solution.py:77
  405.3 9.3 %copy.21 = f32[128,128,128]{2,0,1:T(8,128)} copy(f32[128,128,128]{1,2,0:T(8,128)} %fusion.17) | data formatting | bytes 16777216 | tf_op jit(solution)/shard_map/kab,kah->kbh/dot_general | solution.py:77
  414.6 0.0 copy-start.2
  414.6 6.8 fusion.31
  421.4 2.6 copy.22
  424.0 0.0 reduce-scatter.5.cloned.1.call-update
  424.0 0.0 all-reduce.4.cloned.1.call-start
  424.0 76.6 %psum.15 = f32[128]{0:T(128)} all-reduce(f32[128]{0:T(128)S(1)} %get-tuple-element.7), channel_id=1, replica_groups=mesh['row'=16,'col'=16] {'row','col'}, use_global_device_ids=true, to_apply=%region_8.10 | all-reduce | flops 128 | bytes 1024 | tf_op jit(solution)/shard_map/psum | solution.py:74
  500.6 0.0 copy-done.2
  500.6 1.1 fusion.23
  501.7 0.0 all-reduce.4.cloned.1.call-update
  501.7 0.0 reduce-scatter.5.cloned.1.call-done
  501.8 1.7 broadcast_multiply_fusion
  503.4 252.8 %all-reduce.4.cloned.1.call-done = f32[128,128]{1,0:T(8,128)} async-done(((f32[128,128]{1,0:T(8,128)}), f32[128,128]{1,0:T(8,128)}) %all-reduce.4.cloned.1.call-update) | async-done | bytes 65552 | tf_op jit(solution)/shard_map/psum | solution.py:74
  756.2 1.5 copy.27
  (5 shorter events, 0.0 us)
Async XLA Ops:
  7.2 307.1 %copy-start = (f32[128,128]{1,0:T(8,128)S(1)}, f32[128,128]{1,0:T(8,128)}, u32[]{:S(2)}) copy-start(f32[128,128]{1,0:T(8,128)} %param.10) | copy-start | bytes 196612
  7.2 8.4 %copy-start.3 = (s32[1,1,128]{2,1,0:T(1,128)S(1)}, s32[1,1,128]{2,1,0:T(1,128)}, u32[]{:S(2)}) copy-start(s32[1,1,128]{2,1,0:T(1,128)} %param.14) | copy-start | bytes 1540
  7.2 77.0 %copy-start.1 = (f32[256,128]{1,0:T(8,128)S(1)}, f32[256,128]{1,0:T(8,128)}, u32[]{:S(2)}) copy-start(f32[256,128]{1,0:T(8,128)} %param.9) | copy-start | bytes 393220
  7.2 167.1 %all-gather.3.cloned.1.call-start = ((), (), s32[]{:S(2)}) async-start(), calls=%async_computation.2 | async-start | bytes 2228224 | tf_op jit(solution)/shard_map/all_gather | solution.py:49
  85.0 229.3 %reduce-scatter.3.cloned.1.call-start = ((), (), s32[]{:S(2)}) async-start(), calls=%async_computation.3 | async-start | bytes 2228224 | tf_op jit(solution)/shard_map/reduce_scatter | solution.py:69
  211.0 9.4 %copy-start.6 = (u32[256]{0:T(256)S(1)}, u32[256]{0:T(256)}, u32[]{:S(2)}) copy-start(u32[256]{0:T(256)} %constant.56) | copy-start | bytes 3076
  211.0 103.3 %copy-start.4 = (f32[256,128]{1,0:T(8,128)S(1)}, f32[256,128]{1,0:T(8,128)}, u32[]{:S(2)}) copy-start(f32[256,128]{1,0:T(8,128)} %param.12) | copy-start | bytes 393220
  211.0 103.3 %copy-start.5 = (f32[128]{0:T(128)S(1)}, f32[128]{0:T(128)}, u32[]{:S(2)}) copy-start(f32[128]{0:T(128)} %param.11) | copy-start | bytes 1540
  220.3 159.4 %all-gather.5.cloned.1.call-start = ((), (), s32[]{:S(2)}) async-start(), calls=%async_computation.4 | async-start | bytes 2228224 | tf_op jit(solution)/shard_map/all_gather | solution.py:75
  317.2 184.6 %reduce-scatter.5.cloned.1.call-start = ((), (), s32[]{:S(2)}) async-start(), calls=%async_computation.5 | async-start | bytes 2228224 | tf_op jit(solution)/shard_map/reduce_scatter | solution.py:92
  414.6 86.0 %copy-start.2 = (f32[256,128]{1,0:T(8,128)S(1)}, f32[256,128]{1,0:T(8,128)}, u32[]{:S(2)}) copy-start(f32[256,128]{1,0:T(8,128)} %reduce-scatter.3.cloned.1.call-done) | copy-start | bytes 393220
  424.0 332.2 %all-reduce.4.cloned.1.call-start = ((), (), s32[]{:S(2)}) async-start(), calls=%async_computation.6 | async-start | bytes 131072 | tf_op jit(solution)/shard_map/psum | solution.py:74
Sparse Core Ops, SparseCore 0:
  85.1 89.0 all-gather.2
  220.5 93.7 reduce-scatter.2
  317.5 62.1 all-gather.4
  424.1 77.1 reduce-scatter.4
  507.3 248.8 all-reduce.3
where the time goes:
time: 765 us; the launch traced here: 764 us
  waiting for transfers between devices  409 us (53%)
  blocking collectives  232 us (30%)
  matrix products  59 us (8%)
  local copies, waits for them, and re-layouts  38.9 us (5%)
  between operations  15.9 us (2%)
  other arithmetic  8.34 us (1%)
    psum x1, waiting for transfers between devices, local(): weight_grad, bias_grad = lax.psum((weight_part, bias_part), ('row', 'col'))  253 us
    unnamed x2, blocking collectives  156 us
    all_gather x1, waiting for transfers between devices, local(): gathered = lax.all_gather(scaled, 'row', axis=0, tiled=True)  89.2 us
    psum x1, blocking collectives, local(): weight_grad, bias_grad = lax.psum((weight_part, bias_part), ('row', 'col'))  76.6 us
    all_gather x1, waiting for transfers between devices, local(): lax.all_gather(back_rows * dst_scale[:, None], 'col', axis=0, tiled=True)  62.5 us
    dot_general x1, matrix products, local(): jnp.einsum('kab,kbh->kah', adjacency, taken, precision=lax.Precision.HIGH...  21.5 us
    dot_general x1, matrix products, local(): jnp.einsum('kab,kah->kbh', adjacency, taken_back, precision=lax.Precision...  19.7 us
  transfers between devices with their start and end apart: 5, of which 4 were waited for; matrix products, arithmetic and copies ran while one was open for 0% of the time, Pallas kernels for 0%

commit v1 on v0

v1 whole, which is shorter than its diff:
```python
import functools

import jax
import jax.numpy as jnp
from jax import lax
from jax.experimental import pallas as pl
from jax.experimental.pallas import tpu as pltpu
from jax.sharding import PartitionSpec as P

TILE = 128
MESH = pl.DeviceIdType.MESH
F32 = jnp.float32
BF16 = jnp.bfloat16
HIGHEST = lax.Precision.HIGHEST
VMEM_SPEC = pl.BlockSpec(memory_space=pltpu.VMEM)
CHUNK = 8
NT = (((1,), (1,)), ((), ()))
NN = (((1,), (0,)), ((), ()))
TN = (((0,), (0,)), ((), ()))


def remote(src, dst, send_sem, recv_sem, **where):
    return pltpu.make_async_remote_copy(
        src_ref=src,
        dst_ref=dst,
        send_sem=send_sem,
        recv_sem=recv_sem,
        device_id=where,
        device_id_type=MESH,
    )


def xor_peer(index, bit):
    return index + bit - 2 * bit * lax.rem(lax.div(index, bit), 2)


def greet(rows, cols):
    barrier = pltpu.get_barrier_semaphore()
    for peer in rows:
        pl.semaphore_signal(barrier, inc=1, device_id={"row": peer}, device_id_type=MESH)
    for peer in cols:
        pl.semaphore_signal(barrier, inc=1, device_id={"col": peer}, device_id_type=MESH)
    pl.semaphore_wait(barrier, len(rows) + len(cols))


def to_column(row_vector):
    spread = jnp.broadcast_to(row_vector, (TILE, TILE))
    diagonal = lax.broadcasted_iota(jnp.int32, (TILE, TILE), 0) == lax.broadcasted_iota(
        jnp.int32, (TILE, TILE), 1
    )
    return jnp.sum(jnp.where(diagonal, spread, 0.0), axis=1, keepdims=True)


def split_pair(value):
    high = value.astype(BF16)
    low = (value - high.astype(F32)).astype(BF16)
    return jnp.concatenate([high, low], axis=1)


def sort_table(slots, live, by_row):
    tile_row = jnp.floor(slots * (1.0 / 32.0))
    tile_col = slots - 32.0 * tile_row
    lane = lax.broadcasted_iota(jnp.int32, (1, TILE), 1).astype(F32)
    key = jnp.where(live, tile_row * 32.0 + tile_col if by_row else tile_col * 32.0 + tile_row, 2048.0 + lane)
    key_column = to_column(key)
    rank = jnp.sum(jnp.where(key < key_column, 1.0, 0.0), axis=1, keepdims=True)
    place = rank == lax.broadcasted_iota(jnp.int32, (TILE, TILE), 1).astype(F32)
    number = lax.broadcasted_iota(jnp.int32, (TILE, 1), 0).astype(F32)

    def moved(column):
        return jnp.sum(jnp.where(place, column, 0.0), axis=0, keepdims=True).astype(jnp.int32)

    ends = (to_column(tile_row), to_column(tile_col))
    if not by_row:
        ends = ends[::-1]
    return moved(number), moved(ends[0]), moved(ends[1])


def degree_kernel(count_ref, slots_ref, adj_ref, tiles_ref, dst_ref, src_ref, info_ref, row_sums, col_sums):
    step = pl.program_id(0)
    tiles = adj_ref[...].astype(F32).astype(BF16)
    tiles_ref[...] = tiles
    selector = (
        lax.broadcasted_iota(jnp.int32, (CHUNK, CHUNK * TILE), 1) // TILE
        == lax.broadcasted_iota(jnp.int32, (CHUNK, CHUNK * TILE), 0)
    ).astype(F32).astype(BF16)
    wide = jnp.concatenate([tiles[k] for k in range(CHUNK)], axis=1)
    tall = tiles.reshape(CHUNK * TILE, TILE)
    here = pl.ds(pl.multiple_of(step * CHUNK, CHUNK), CHUNK)
    row_sums[here, :] = lax.dot_general(selector, wide, NT, preferred_element_type=F32)
    col_sums[here, :] = lax.dot_general(selector, tall, NN, preferred_element_type=F32)

    @pl.when(step == pl.num_programs(0) - 1)
    def _():
        slots = slots_ref[...].astype(F32)
        lane = lax.broadcasted_iota(jnp.int32, (1, TILE), 1)
        live = lane < count_ref[0, 0]
        tile_row = jnp.floor(slots * (1.0 / 32.0))
        tile_col = slots - 32.0 * tile_row
        tile_number = lax.broadcasted_iota(jnp.int32, (32, TILE), 0).astype(F32)
        row_select = jnp.where(live & (tile_row == tile_number), 1.0, 0.0).astype(BF16)
        col_select = jnp.where(live & (tile_col == tile_number), 1.0, 0.0).astype(BF16)
        dst_ref[...] = jnp.dot(row_select, row_sums[...].astype(BF16), preferred_element_type=F32)
        src_ref[...] = jnp.dot(col_select, col_sums[...].astype(BF16), preferred_element_type=F32)
        info_ref[...] = jnp.zeros_like(info_ref)
        for base, by_row in ((0, True), (4, False)):
            for place, line in enumerate(sort_table(slots, live, by_row)):
                info_ref[base + place : base + place + 1, :] = line


def block_degrees(adj_tiles, slots, count):
    slot_total = adj_tiles.shape[0]
    return pl.pallas_call(
        degree_kernel,
        grid=(slot_total // CHUNK,),
        in_specs=[
            pl.BlockSpec(memory_space=pltpu.SMEM),
            pl.BlockSpec((1, TILE), lambda i: (0, 0)),
            pl.BlockSpec((CHUNK, TILE, TILE), lambda i: (i, 0, 0)),
        ],
        out_specs=[
            pl.BlockSpec((CHUNK, TILE, TILE), lambda i: (i, 0, 0)),
            pl.BlockSpec((32, TILE), lambda i: (0, 0)),
            pl.BlockSpec((32, TILE), lambda i: (0, 0)),
            pl.BlockSpec((8, TILE), lambda i: (0, 0)),
        ],
        out_shape=[
            jax.ShapeDtypeStruct((slot_total, TILE, TILE), BF16),
            jax.ShapeDtypeStruct((32, TILE), F32),
            jax.ShapeDtypeStruct((32, TILE), F32),
            jax.ShapeDtypeStruct((8, TILE), jnp.int32),
        ],
        scratch_shapes=[pltpu.VMEM((TILE, TILE), F32), pltpu.VMEM((TILE, TILE), F32)],
        name="block_degrees",
    )(count, slots, adj_tiles)


def product_kernel(dims, count_ref, info_ref, tiles_ref, pair_ref, out_ref):
    unroll = 8
    count = count_ref[0, 0]
    out_ref[...] = jnp.zeros_like(out_ref)

    def body(step, total):
        for u in range(unroll):
            k = step * unroll + u
            at = jnp.minimum(k, count - 1)
            before = jnp.maximum(at - 1, 0)
            target = info_ref[1, at]
            both = lax.dot_general(
                tiles_ref[info_ref[0, at]], pair_ref[info_ref[2, at]], dims, preferred_element_type=F32
            )
            product = both[:, :TILE] + both[:, TILE:]
            goes_on = (k > 0) & (info_ref[1, before] == target)
            joined = product + jnp.where(goes_on, total, 0.0)
            total = jnp.where(k < count, joined, total)
            out_ref[target] = total
        return total

    lax.fori_loop(0, lax.div(count + unroll - 1, unroll), body, jnp.zeros((TILE, TILE), F32))


def sparse_product(dims, count, info, tiles, pairs, name):
    return pl.pallas_call(
        functools.partial(product_kernel, dims),
        in_specs=[pl.BlockSpec(memory_space=pltpu.SMEM)] * 2 + [VMEM_SPEC] * 2,
        out_specs=VMEM_SPEC,
        out_shape=jax.ShapeDtypeStruct((32, TILE, TILE), F32),
        name=name,
    )(count, info, tiles, pairs)


LINE = ((0, 0), (1, -1), (1, 1), (2, -1), (2, 1), (3, -1), (3, 1))


def gather_kernel(
    feat_ref, src_ref, dst_ref, pair_ref, src_scale_ref, dst_scale_ref,
    held, deg_sent, deg_got, recv_sem, z_sem, y_sem, relay_sem, deg_send_sem, deg_recv_sem,
):
    row, col = lax.axis_index("row"), lax.axis_index("col")
    y, z = lax.div(row, 4), lax.rem(row, 4)
    y_up, y_down, y_far = lax.rem(y + 1, 4), lax.rem(y + 3, 4), lax.rem(y + 2, 4)
    greet(
        [lax.rem(y + d, 4) * 4 + z for d in (1, 2, 3)] + [y * 4 + lax.rem(z + d, 4) for d in (1, 2, 3)],
        [xor_peer(col, bit) for bit in (1, 2, 4, 8)],
    )

    def own(z_from, half):
        if z_from is None:
            return feat_ref.at[half]
        return held.at[y * 4 + z_from, half]

    def z_copy(z_from, first, way, half):
        block = y * 4 + z_from
        return remote(
            own(None if first else z_from, half), held.at[block, half],
            z_sem.at[z_from, way, half], recv_sem.at[block, half],
            row=y * 4 + lax.rem(z + (1 if way == 0 else 3), 4),
        )

    def y_copy(z_from, first, way, half):
        block = y * 4 + z_from
        return remote(
            own(None if first else z_from, half), held.at[block, half],
            y_sem.at[z_from, way, half], recv_sem.at[block, half],
            row=(y_up if way == 0 else y_down) * 4 + z,
        )

    def relay_copy(z_from, half):
        block = (y_down if half == 0 else y_up) * 4 + z_from
        return remote(
            held.at[block, half], held.at[block, half],
            relay_sem.at[z_from, half], recv_sem.at[block, half],
            row=(y_up if half == 0 else y_down) * 4 + z,
        )

    def arrived(block, half):
        remote(
            held.at[block, half], held.at[block, half], relay_sem.at[0, half], recv_sem.at[block, half],
            row=y_up * 4 + z,
        ).wait_recv()

    def here(distance, sign):
        return (z + sign * distance >= 0) & (z + sign * distance <= 3)

    def on_way(distance, sign, action):
        z_from = z + sign * distance
        for way, goes in ((0, z < 3), (1, z > 0)):
            if distance and (way == 0) != (sign < 0):
                continue

            @pl.when(goes)
            def _():
                for half in (0, 1):
                    action(z_copy(z_from, distance == 0, way, half))

    def column_step(distance, sign):
        z_from = z + sign * distance
        if distance:
            for half in (0, 1):
                arrived(y * 4 + z_from, half)
        for half in (0, 1):
            for way in (0, 1):
                y_copy(z_from, distance == 0, way, half).start()
        on_way(distance, sign, lambda copy: copy.start())

    def relay_step(distance, sign):
        z_from = z + sign * distance
        for half in (0, 1):
            arrived((y_down if half == 0 else y_up) * 4 + z_from, half)
            relay_copy(z_from, half).start()

    def degree_copy(which, step):
        source = (src_ref, dst_ref)[which] if step == 0 else deg_sent.at[which, step - 1]
        where = {("row", "col")[which]: xor_peer((row, col)[which], 1 << step)}
        return remote(
            source, deg_got.at[which, step], deg_send_sem.at[which, step], deg_recv_sem.at[which, step], **where
        )

    def degree_step(step):
        for which in (0, 1):
            copy = degree_copy(which, step)
            copy.wait_recv()
            source = (src_ref, dst_ref)[which] if step == 0 else deg_sent.at[which, step - 1]
            deg_sent[which, step] = source[...] + deg_got[which, step]
            if step < 3:
                degree_copy(which, step + 1).start()

    for which in (0, 1):
        degree_copy(which, 0).start()
    column_step(0, 0)
    held[row] = feat_ref[...]
    degree_step(0)
    for place, (distance, sign) in enumerate(LINE[1:]):
        pl.when(here(distance, sign))(functools.partial(column_step, distance, sign))
        before = LINE[place]
        pl.when(here(*before))(functools.partial(relay_step, *before))
        if place in (1, 3, 5):
            degree_step(1 + place // 2)
    pl.when(here(*LINE[-1]))(functools.partial(relay_step, *LINE[-1]))

    src_scale = lax.rsqrt(1.0 + deg_sent[0, 3])
    src_scale_ref[...] = src_scale
    dst_scale_ref[...] = lax.rsqrt(1.0 + deg_sent[1, 3])

    def settle(block):
        for half in (0, 1):
            tile = 2 * block + half
            scale = to_column(src_scale_ref[pl.ds(tile, 1), :])
            pair_ref[tile] = split_pair(held[block, half] * scale)

    for z_from in range(4):
        settle(y * 4 + z_from)

    def last_step(distance, sign):
        z_from = z + sign * distance
        arrived(y_down * 4 + z_from, 1)
        settle(y_down * 4 + z_from)
        arrived(y_up * 4 + z_from, 0)
        settle(y_up * 4 + z_from)

    def far_step(distance, sign):
        z_from = z + sign * distance
        arrived(y_far * 4 + z_from, 0)
        arrived(y_far * 4 + z_from, 1)
        settle(y_far * 4 + z_from)

    def send_step(distance, sign):
        z_from = z + sign * distance
        for half in (0, 1):
            for way in (0, 1):
                y_copy(z_from, distance == 0, way, half).wait_send()
            relay_copy(z_from, half).wait_send()
        on_way(distance, sign, lambda copy: copy.wait_send())

    for action in (last_step, far_step, send_step):
        for item in LINE:
            pl.when(here(*item))(functools.partial(action, *item))
    for which in (0, 1):
        for step in range(4):
            degree_copy(which, step).wait_send()


def gather_features(features, src_part, dst_part):
    dma = pltpu.SemaphoreType.DMA
    return pl.pallas_call(
        gather_kernel,
        in_specs=[VMEM_SPEC] * 3,
        out_specs=[VMEM_SPEC] * 3,
        out_shape=[
            jax.ShapeDtypeStruct((32, TILE, 2 * TILE), BF16),
            jax.ShapeDtypeStruct((32, TILE), F32),
            jax.ShapeDtypeStruct((32, TILE), F32),
        ],
        scratch_shapes=[
            pltpu.VMEM((16, 2, TILE, TILE), F32),
            pltpu.VMEM((2, 4, 32, TILE), F32),
            pltpu.VMEM((2, 4, 32, TILE), F32),
            dma((16, 2)),
            dma((4, 2, 2)),
            dma((4, 2, 2)),
            dma((4, 2)),
            dma((2, 4)),
            dma((2, 4)),
        ],
        compiler_params=pltpu.CompilerParams(collective_id=0, has_side_effects=True),
        name="gather_features",
    )(features.reshape(2, TILE, TILE), src_part, dst_part)


WROWS = 72


def layer_kernel(
    part_ref, w_ref, b_ref, grad_ref, scale_ref, act_ref, pair_ref, wsum_ref,
    sib_got, ring_a, ring_b, from_left, from_right, z_sent, z_got, held, wgrad, w_sent, w_got,
    sib_ssem, sib_rsem, far_ssem, far_rsem, near_ssem, near_rsem, z_ssem, z_rsem,
    recv_sem, zg_sem, xg_sem, relay_sem, sg_sem, w_ssem, w_rsem,
):
    col = lax.axis_index("col")
    x, zh, core = lax.div(col, 4), lax.rem(lax.div(col, 2), 2), lax.rem(col, 2)
    x_up, x_down, x_far = lax.rem(x + 1, 4), lax.rem(x + 3, 4), lax.rem(x + 2, 4)
    sibling = col + 1 - 2 * core
    z_peer = col + 2 - 4 * zh
    up, down = x_up * 4 + zh * 2 + core, x_down * 4 + zh * 2 + core
    greet([], [sibling, z_peer, up, down, x_far * 4 + zh * 2 + core])

    def sib_copy(place, which):
        target = (x_far, x_up, x_down, x)[place]
        half_z = 1 - zh if which == 0 else zh
        return remote(
            part_ref.at[target * 4 + half_z * 2 + 1 - core], sib_got.at[place, which],
            sib_ssem.at[place, which], sib_rsem.at[place, which], col=sibling,
        )

    def far_copy(which, way):
        return remote(
            sib_got.at[0, which, way], (ring_a, ring_b)[way].at[which],
            far_ssem.at[which, way], far_rsem.at[which, way], col=(up, down)[way],
        )

    def near_copy(which, way, half):
        return remote(
            sib_got.at[1 + way, which, half], (from_left, from_right)[way].at[which, half],
            near_ssem.at[which, way, half], near_rsem.at[which, way, half], col=(up, down)[way],
        )

    def z_copy(half):
        return remote(z_sent.at[half], z_got.at[half], z_ssem.at[half], z_rsem.at[half], col=z_peer)

    def join(place, which):
        target = (x_far, x_up, x_down, x)[place]
        half_z = 1 - zh if which == 0 else zh
        sib_copy(place, which).wait_recv()
        sib_got[place, which] += part_ref[target * 4 + half_z * 2 + core]

    for which in (0, 1):
        for place in range(4):
            sib_copy(place, which).start()
    for which in (0, 1):
        join(0, which)
        for way in (0, 1):
            far_copy(which, way).start()
        for way in (0, 1):
            join(1 + way, which)
            near_copy(which, way, 1 - way).start()
    for which in (0, 1):
        for way in (0, 1):
            far_copy(which, way).wait_recv()
            sib_got[1 + way, which, way] += (ring_a, ring_b)[way][which]
            near_copy(which, way, way).start()
    for which in (0, 1):
        join(3, which)
        for half in (1, 0):
            for way in (0, 1):
                near_copy(which, way, half).wait_recv()
            total = sib_got[3, which, half] + from_left[which, half] + from_right[which, half]
            if which == 0:
                z_sent[half] = total
                z_copy(half).start()
            else:
                sib_got[3, which, half] = total
    for half in (0, 1):
        z_copy(half).wait_recv()

    scales, pre_grads, rows = [], [], []
    for half in (0, 1):
        scale = to_column(scale_ref[pl.ds(2 * col + half, 1), :])
        rows.append((sib_got[3, 1, half] + z_got[half]) * scale)
        scales.append(scale)
    aggregated = jnp.concatenate(rows, axis=0)
    scale = jnp.concatenate(scales, axis=0)
    preact = jnp.dot(aggregated, w_ref[...], precision=HIGHEST, preferred_element_type=F32) + b_ref[...]
    logistic = 1.0 / (1.0 + jnp.exp(-preact))
    act_ref[...] = preact * logistic
    pre_grad = grad_ref[...] * logistic * (1.0 + preact * (1.0 - logistic))
    back = lax.dot_general(pre_grad, w_ref[...], NT, precision=HIGHEST, preferred_element_type=F32) * scale
    held[col, 0] = back[:TILE]
    held[col, 1] = back[TILE:]

    def spread_z(half):
        return remote(
            held.at[col, half], held.at[col, half], zg_sem.at[half], recv_sem.at[col, half], col=z_peer
        )

    def spread_x(which, way, half):
        half_z = zh if which == 0 else 1 - zh
        block = x * 4 + half_z * 2 + core
        return remote(
            held.at[block, half], held.at[block, half], xg_sem.at[which, way, half], recv_sem.at[block, half],
            col=(up, down)[way],
        )

    def relay_x(which, half):
        half_z = zh if which == 0 else 1 - zh
        block = (x_down if half == 0 else x_up) * 4 + half_z * 2 + core
        return remote(
            held.at[block, half], held.at[block, half], relay_sem.at[which, half], recv_sem.at[block, half],
            col=(up, down)[half],
        )

    def spread_sib(place, which, half):
        target = (x, x_up, x_down, x_far)[place]
        half_z = zh if which == 0 else 1 - zh
        block = target * 4 + half_z * 2 + core
        return remote(
            held.at[block, half], held.at[block, half], sg_sem.at[place, which, half], recv_sem.at[block, half],
            col=sibling,
        )

    def arrived(block, half):
        remote(
            held.at[block, half], held.at[block, half], zg_sem.at[half], recv_sem.at[block, half], col=sibling
        ).wait_recv()

    def settle(block, half):
        pair_ref[2 * block + half] = split_pair(held[block, half])

    for half in (0, 1):
        spread_z(half).start()
    for half in (0, 1):
        for way in (0, 1):
            spread_x(0, way, half).start()
    for half in (0, 1):
        spread_sib(0, 0, half).start()

    wgrad[0:TILE, :] = lax.dot_general(aggregated, pre_grad, TN, precision=HIGHEST, preferred_element_type=F32)
    first_row = lax.broadcasted_iota(jnp.int32, (16, TILE), 0) == 0
    wgrad[TILE : TILE + 16, :] = jnp.where(first_row, jnp.sum(pre_grad, axis=0, keepdims=True), 0.0)

    def w_rows(which):
        return pl.ds(pl.multiple_of(which * WROWS, 8), WROWS)

    def w_copy(step):
        if step == 0:
            return remote(
                wgrad.at[w_rows(1 - core)], w_got.at[0], w_ssem.at[0], w_rsem.at[0], col=sibling
            )
        peer = xor_peer(col, 1 << step)
        return remote(w_sent.at[step - 1], w_got.at[step], w_ssem.at[step], w_rsem.at[step], col=peer)

    def w_step(step):
        w_copy(step).wait_recv()
        mine = wgrad[w_rows(core), :] if step == 0 else w_sent[step - 1]
        total = mine + w_got[step]
        if step < 3:
            w_sent[step] = total
            w_copy(step + 1).start()
        else:
            wsum_ref[...] = total

    def relay(which):
        half_z = zh if which == 0 else 1 - zh
        for half in (0, 1):
            side = x_down if half == 0 else x_up
            arrived(side * 4 + half_z * 2 + core, half)
            relay_x(which, half).start()
            spread_sib((2, 1)[half], which, half).start()

    def near_rest(which):
        half_z = zh if which == 0 else 1 - zh
        for half in (0, 1):
            side = x_up if half == 0 else x_down
            arrived(side * 4 + half_z * 2 + core, half)
            spread_sib((1, 2)[half], which, half).start()

    def far_rest(which):
        half_z = zh if which == 0 else 1 - zh
        for half in (0, 1):
            arrived(x_far * 4 + half_z * 2 + core, half)
            spread_sib(3, which, half).start()

    w_copy(0).start()
    relay(0)
    near_rest(0)
    w_step(0)
    other = x * 4 + (1 - zh) * 2 + core
    for half in (0, 1):
        arrived(other, half)
        for way in (0, 1):
            spread_x(1, way, half).start()
        spread_sib(0, 1, half).start()
    far_rest(0)
    w_step(1)
    for side in (x, x_up, x_down, x_far):
        for half in (0, 1):
            settle(side * 4 + zh * 2 + core, half)
    relay(1)
    near_rest(1)
    w_step(2)
    for side in (x, x_up, x_down, x_far):
        for half in (0, 1):
            block = side * 4 + zh * 2 + 1 - core
            arrived(block, half)
            settle(block, half)
    far_rest(1)
    w_step(3)
    for side in (x, x_up, x_down, x_far):
        for half in (0, 1):
            settle(side * 4 + (1 - zh) * 2 + core, half)
    for side in (x, x_up, x_down, x_far):
        for half in (0, 1):
            block = side * 4 + (1 - zh) * 2 + 1 - core
            arrived(block, half)
            settle(block, half)

    for which in (0, 1):
        for place in range(4):
            sib_copy(place, which).wait_send()
            for half in (0, 1):
                spread_sib(place, which, half).wait_send()
        for way in (0, 1):
            far_copy(which, way).wait_send()
            relay_x(which, way).wait_send()
            for half in (0, 1):
                near_copy(which, way, half).wait_send()
                spread_x(which, way, half).wait_send()
    for half in (0, 1):
        z_copy(half).wait_send()
        spread_z(half).wait_send()
    for step in range(4):
        w_copy(step).wait_send()


def dense_layer(part, weight, bias_vector, out_grad, dst_scale):
    dma = pltpu.SemaphoreType.DMA
    half = (TILE, TILE)
    return pl.pallas_call(
        layer_kernel,
        in_specs=[VMEM_SPEC] * 5,
        out_specs=[VMEM_SPEC] * 3,
        out_shape=[
            jax.ShapeDtypeStruct((2 * TILE, TILE), F32),
            jax.ShapeDtypeStruct((32, TILE, 2 * TILE), BF16),
            jax.ShapeDtypeStruct((WROWS, TILE), F32),
        ],
        scratch_shapes=[
            pltpu.VMEM((4, 2, 2) + half, F32),
            pltpu.VMEM((2,) + half, F32),
            pltpu.VMEM((2,) + half, F32),
            pltpu.VMEM((2, 2) + half, F32),
            pltpu.VMEM((2, 2) + half, F32),
            pltpu.VMEM((2,) + half, F32),
            pltpu.VMEM((2,) + half, F32),
            pltpu.VMEM((16, 2) + half, F32),
            pltpu.VMEM((2 * WROWS, TILE), F32),
            pltpu.VMEM((3, WROWS, TILE), F32),
            pltpu.VMEM((4, WROWS, TILE), F32),
            dma((4, 2)), dma((4, 2)), dma((2, 2)), dma((2, 2)), dma((2, 2, 2)), dma((2, 2, 2)), dma((2,)), dma((2,)),
            dma((16, 2)), dma((2,)), dma((2, 2, 2)), dma((2, 2)), dma((4, 2, 2)), dma((4,)), dma((4,)),
        ],
        compiler_params=pltpu.CompilerParams(collective_id=1, has_side_effects=True),
        name="dense_layer",
    )(part.reshape((16, 2) + half), weight, bias_vector.reshape(1, TILE), out_grad, dst_scale)


def scatter_kernel(
    part_ref, wsum_ref, scale_ref, grad_ref, wgrad_ref,
    staged_a, staged_b, ring_a, ring_b, from_down, from_up, total, line_up, line_down, w_sent, w_got, w_all,
    far_ssem, far_rsem, near_ssem, near_rsem, line_ssem, line_rsem, w_ssem, w_rsem,
):
    row, col = lax.axis_index("row"), lax.axis_index("col")
    y, z = lax.div(row, 4), lax.rem(row, 4)
    core = lax.rem(col, 2)
    y_up, y_down, y_far = lax.rem(y + 1, 4), lax.rem(y + 3, 4), lax.rem(y + 2, 4)
    sibling = col + 1 - 2 * core
    greet(
        [lax.rem(y + d, 4) * 4 + z for d in (1, 2, 3)] + [y * 4 + lax.rem(z + d, 4) for d in (1, 2, 3)],
        [sibling],
    )
    up, down = y_up * 4 + z, y_down * 4 + z

    def here(distance, sign):
        return (z + sign * distance >= 0) & (z + sign * distance <= 3)

    def far_copy(zb, way):
        return remote(
            part_ref.at[y_far * 4 + zb, way], (ring_a, ring_b)[way].at[zb],
            far_ssem.at[zb, way], far_rsem.at[zb, way], row=(up, down)[way],
        )

    def near_copy(zb, way, half):
        block = (y_up, y_down)[way] * 4 + zb
        source = (staged_a, staged_b)[way].at[zb] if half == way else part_ref.at[block, half]
        return remote(
            source, (from_down, from_up)[way].at[zb, half],
            near_ssem.at[zb, way, half], near_rsem.at[zb, way, half], row=(up, down)[way],
        )

    def line_copy(zb, way, half):
        return remote(
            total.at[zb, half], (line_up, line_down)[way].at[zb, half],
            line_ssem.at[zb, half], line_rsem.at[zb, way, half], row=y * 4 + lax.rem(z + (1 if way == 0 else 3), 4),
        )

    def w_copy(step):
        if step == 4:
            return remote(w_sent.at[3], w_all, w_ssem.at[4], w_rsem.at[4], col=sibling)
        source = wsum_ref if step == 0 else w_sent.at[step - 1]
        return remote(source, w_got.at[step], w_ssem.at[step], w_rsem.at[step], row=xor_peer(row, 1 << step))

    def w_step(step):
        w_copy(step).wait_recv()
        source = wsum_ref if step == 0 else w_sent.at[step - 1]
        w_sent[step] = source[...] + w_got[step]
        w_copy(step + 1).start()

    def open_step(distance, sign):
        zb = z + sign * distance
        for way in (0, 1):
            far_copy(zb, way).start()
        for way in (0, 1):
            near_copy(zb, way, 1 - way).start()

    def relay_step(distance, sign):
        zb = z + sign * distance
        for way in (0, 1):
            far_copy(zb, way).wait_recv()
            block = (y_up, y_down)[way] * 4 + zb
            (staged_a, staged_b)[way][zb] = part_ref[block, way] + (ring_a, ring_b)[way][zb]
            near_copy(zb, way, way).start()

    def close_step(distance, sign):
        zb = z + sign * distance
        for half in (0, 1):
            for way in (0, 1):
                near_copy(zb, way, half).wait_recv()
            total[zb, half] = part_ref[y * 4 + zb, half] + from_down[zb, half] + from_up[zb, half]

        def collect(way):
            for half in (0, 1):
                line_copy(zb, way, half).wait_recv()
                total[zb, half] += (line_up, line_down)[way][zb, half]

        if distance == 0:
            pl.when(z > 0)(functools.partial(collect, 0))
            pl.when(z < 3)(functools.partial(collect, 1))
        else:
            way = 0 if sign > 0 else 1
            pl.when(z > 0 if way == 0 else z < 3)(functools.partial(collect, way))
            for half in (0, 1):
                line_copy(zb, way, half).start()

    def send_step(distance, sign):
        zb = z + sign * distance
        for way in (0, 1):
            far_copy(zb, way).wait_send()
            for half in (0, 1):
                near_copy(zb, way, half).wait_send()
        if distance:
            for half in (0, 1):
                line_copy(zb, 0 if sign > 0 else 1, half).wait_send()

    backwards = LINE[::-1]
    for item in backwards:
        pl.when(here(*item))(functools.partial(open_step, *item))
    w_copy(0).start()
    for place, item in enumerate(backwards):
        pl.when(here(*item))(functools.partial(relay_step, *item))
        if place >= 1:
            before = backwards[place - 1]
            pl.when(here(*before))(functools.partial(close_step, *before))
        if place in (2, 3, 4, 6):
            w_step((2, 3, 4, 6).index(place))
    close_step(*backwards[-1])

    for half in (0, 1):
        scale = to_column(scale_ref[pl.ds(2 * row + half, 1), :])
        grad_ref[pl.ds(half * TILE, TILE), :] = total[z, half] * scale
    w_copy(4).wait_recv()
    wgrad_ref[pl.ds(pl.multiple_of(core * WROWS, 8), WROWS), :] = w_sent[3]
    wgrad_ref[pl.ds(pl.multiple_of((1 - core) * WROWS, 8), WROWS), :] = w_all[...]
    for item in backwards:
        pl.when(here(*item))(functools.partial(send_step, *item))
    for step in range(5):
        w_copy(step).wait_send()


def scatter_gradients(part, wsum, src_scale):
    dma = pltpu.SemaphoreType.DMA
    half = (TILE, TILE)
    return pl.pallas_call(
        scatter_kernel,
        in_specs=[VMEM_SPEC] * 3,
        out_specs=[VMEM_SPEC] * 2,
        out_shape=[
            jax.ShapeDtypeStruct((2 * TILE, TILE), F32),
            jax.ShapeDtypeStruct((2 * WROWS, TILE), F32),
        ],
        scratch_shapes=[
            pltpu.VMEM((4,) + half, F32),
            pltpu.VMEM((4,) + half, F32),
            pltpu.VMEM((4,) + half, F32),
            pltpu.VMEM((4,) + half, F32),
            pltpu.VMEM((4, 2) + half, F32),
            pltpu.VMEM((4, 2) + half, F32),
            pltpu.VMEM((4, 2) + half, F32),
            pltpu.VMEM((4, 2) + half, F32),
            pltpu.VMEM((4, 2) + half, F32),
            pltpu.VMEM((4, WROWS, TILE), F32),
            pltpu.VMEM((4, WROWS, TILE), F32),
            pltpu.VMEM((WROWS, TILE), F32),
            dma((4, 2)), dma((4, 2)), dma((4, 2, 2)), dma((4, 2, 2)), dma((4, 2)), dma((4, 2, 2)), dma((5,)), dma((5,)),
        ],
        compiler_params=pltpu.CompilerParams(collective_id=2, has_side_effects=True),
        name="scatter_gradients",
    )(part.reshape((16, 2) + half), wsum, src_scale)


def local(features, weight, bias_vector, out_grad, adj_tiles, tile_slots, tile_counts):
    tiles, dst_part, src_part, info = block_degrees(adj_tiles[0, 0], tile_slots[0], tile_counts)
    pairs, src_scale, dst_scale = gather_features(features, src_part, dst_part)
    part = sparse_product(NN, tile_counts, info[:4], tiles, pairs, "forward_product")
    activated, grad_pairs, wsum = dense_layer(part, weight, bias_vector, out_grad, dst_scale)
    back = sparse_product(TN, tile_counts, info[4:], tiles, grad_pairs, "backward_product")
    feature_grad, wgrad = scatter_gradients(back, wsum, src_scale)
    return activated, feature_grad, wgrad[:TILE], wgrad[TILE]


def solution(mesh):
    return jax.shard_map(
        local,
        mesh=mesh,
        in_specs=(
            P(("col", "row"), None),
            P(),
            P(),
            P(("row", "col"), None),
            P("row", "col", None, None, None),
            P("row", "col", None),
            P("row", "col"),
        ),
        out_specs=(P(("row", "col"), None), P(("col", "row"), None), P(), P()),
        check_vma=False,
    )
```

time: 765 us -> 152 us (0.20)
  the two profiles are of different devices: /device:TPU:1 before, /device:TPU:2 now
where the time goes in v1:
time: 152 us; the launch traced here: 149 us
  Pallas kernels  142 us (93%)
  local copies, waits for them, and re-layouts  6.25 us (4%)
    pallas_call x1, Pallas kernels, dense_layer(): pl.pallas_call(layer_kernel, in_specs=[VMEM_SPEC] * 5, out_specs=[VMEM_SP...  43 us
    pallas_call x1, Pallas kernels, gather_features(): pl.pallas_call(gather_kernel, in_specs=[VMEM_SPEC] * 3, out_specs=[VMEM_S...  37.7 us
    pallas_call x1, Pallas kernels, scatter_gradients(): pl.pallas_call(scatter_kernel, in_specs=[VMEM_SPEC] * 3, out_specs=[VMEM_...  35.1 us
    pallas_call x2, Pallas kernels, sparse_product(): pl.pallas_call(functools.partial(product_kernel, dims), in_specs=[pl.Bloc...  13.2 us
    pallas_call x1, Pallas kernels, block_degrees(): pl.pallas_call(degree_kernel, grid=(slot_total // CHUNK,), in_specs=[pl.B...  12.6 us

profile of v1, /device:TPU:2, one launch (start us, length us, event | category | flops | bytes accessed | tf_op | source)
XLA Modules:
  0.0 149.2 jit_solution(9938555716532244184)
XLA Ops:
  1.3 12.6 %block_degrees.1 = (bf16[128,128,128]{2,1,0:T(8,128)(2,1)}, f32[32,128]{1,0:T(8,128)}, f32[32,128]{1,0:T(8,128)}, s32[8,128]{1,0:T(8,128)}) custom-call(s32[1,1]{1,0:T(1,128)S(6)} %copy.13.count_ref, s32[1,128]{1,0:T(1,128)} %bitcast.12, s32[128,128,128]{2,1,0:T(8,128)} %bitcast.10), custom_call_target="tpu_custom_call" | custom-call | tf_op jit(solution)/shard_map/block_degrees/pallas_call | solution.py:113
  13.9 1.4 fusion
  15.3 37.7 %gather_features.1 = (bf16[32,128,256]{2,1,0:T(8,128)(2,1)}, f32[32,128]{1,0:T(8,128)}, f32[32,128]{1,0:T(8,128)}) custom-call(f32[2,128,128]{2,1,0:T(8,128)} %bitcast.11, f32[32,128]{1,0:T(8,128)} %get-tuple-element.18.src_ref, f32[32,128]{1,0:T(8,128)} %get-tuple-element.19.dst_ref), custom_call_target="tpu_custom_call" | custom-call | tf_op jit(solution)/shard_map/gather_features/pallas_call | solution.py:325
  53.0 6.5 %forward_product.1 = f32[32,128,128]{2,1,0:T(8,128)} custom-call(s32[1,1]{1,0:T(1,128)S(6)} %copy.13.count_ref, s32[4,128]{1,0:T(4,128)} %get-tuple-element.29.info_ref, bf16[128,128,128]{2,1,0:T(8,128)(2,1)} %get-tuple-element.17.tiles_ref, bf16[32,128,256]{2,1,0:T(8,128)(2,1)} %get-tuple-element.20.pair_ref), custom_call_target="tpu_custom_call" | custom-call | tf_op jit(solution)/shard_map/forward_product/pallas_call | solution.py:163
  59.4 43.0 %dense_layer.1 = (f32[256,128]{1,0:T(8,128)}, bf16[32,128,256]{2,1,0:T(8,128)(2,1)}, f32[72,128]{1,0:T(8,128)}) custom-call(f32[16,2,128,128]{3,2,1,0:T(8,128)} %bitcast.8, f32[128,128]{1,0:T(8,128)} %w_ref.1, f32[1,128]{1,0:T(1,128)} %bitcast.13, f32[256,128]{1,0:T(8,128)} %grad_ref.1, f32[32,128]{1,0:T(8,128)} %get-tuple-element.21.scale_ref), custom_call_target="tpu_custom_call" | custom-call | tf_op jit(solution)/shard_map/dense_layer/pallas_call | solution.py:587
  102.4 6.7 %backward_product.1 = f32[32,128,128]{2,1,0:T(8,128)} custom-call(s32[1,1]{1,0:T(1,128)S(6)} %copy.13.count_ref, s32[4,128]{1,0:T(4,128)} %get-tuple-element.28.info_ref, bf16[128,128,128]{2,1,0:T(8,128)(2,1)} %get-tuple-element.17.tiles_ref, bf16[32,128,256]{2,1,0:T(8,128)(2,1)} %get-tuple-element.23.pair_ref), custom_call_target="tpu_custom_call" | custom-call | tf_op jit(solution)/shard_map/backward_product/pallas_call | solution.py:163
  109.1 0.0 copy-start
  109.1 35.1 %scatter_gradients.1 = (f32[256,128]{1,0:T(8,128)}, f32[144,128]{1,0:T(8,128)}) custom-call(f32[16,2,128,128]{3,2,1,0:T(8,128)} %bitcast.9, f32[72,128]{1,0:T(8,128)} %get-tuple-element.24.wsum_ref, f32[32,128]{1,0:T(8,128)} %get-tuple-element.25.scale_ref), custom_call_target="tpu_custom_call" | custom-call | tf_op jit(solution)/shard_map/scatter_gradients/pallas_call | solution.py:741
  144.3 1.2 slice_bitcast_fusion
  145.5 1.5 slice.14
  146.9 0.0 copy-done
  146.9 0.7 copy.14
  147.6 1.6 %copy.15 = f32[256,128]{1,0:T(8,128)} copy(f32[256,128]{1,0:T(8,128)} %get-tuple-element.35) | data formatting | bytes 262144
Async XLA Ops:
  109.1 37.8 %copy-start = (f32[256,128]{1,0:T(8,128)S(1)}, f32[256,128]{1,0:T(8,128)}, u32[]{:S(2)}) copy-start(f32[256,128]{1,0:T(8,128)} %get-tuple-element.34) | copy-start | bytes 393220

commit v2 on v1

--- a/solution.py
+++ b/solution.py
@@ -14,6 +14,8 @@
 HIGHEST = lax.Precision.HIGHEST
 VMEM_SPEC = pl.BlockSpec(memory_space=pltpu.VMEM)
 CHUNK = 8
+BY_WAY = ((0, 0), (1, 1), (0, 1), (1, 0))
+LIMIT = 24 << 20
 NT = (((1,), (1,)), ((), ()))
 NN = (((1,), (0,)), ((), ()))
 TN = (((0,), (0,)), ((), ()))
@@ -40,7 +42,7 @@
         pl.semaphore_signal(barrier, inc=1, device_id={"row": peer}, device_id_type=MESH)
     for peer in cols:
         pl.semaphore_signal(barrier, inc=1, device_id={"col": peer}, device_id_type=MESH)
-    pl.semaphore_wait(barrier, len(rows) + len(cols))
+    return lambda: pl.semaphore_wait(barrier, len(rows) + len(cols))
 
 
 def to_column(row_vector):
@@ -74,65 +76,6 @@
     if not by_row:
         ends = ends[::-1]
     return moved(number), moved(ends[0]), moved(ends[1])
-
-
-def degree_kernel(count_ref, slots_ref, adj_ref, tiles_ref, dst_ref, src_ref, info_ref, row_sums, col_sums):
-    step = pl.program_id(0)
-    tiles = adj_ref[...].astype(F32).astype(BF16)
-    tiles_ref[...] = tiles
-    selector = (
-        lax.broadcasted_iota(jnp.int32, (CHUNK, CHUNK * TILE), 1) // TILE
-        == lax.broadcasted_iota(jnp.int32, (CHUNK, CHUNK * TILE), 0)
-    ).astype(F32).astype(BF16)
-    wide = jnp.concatenate([tiles[k] for k in range(CHUNK)], axis=1)
-    tall = tiles.reshape(CHUNK * TILE, TILE)
-    here = pl.ds(pl.multiple_of(step * CHUNK, CHUNK), CHUNK)
-    row_sums[here, :] = lax.dot_general(selector, wide, NT, preferred_element_type=F32)
-    col_sums[here, :] = lax.dot_general(selector, tall, NN, preferred_element_type=F32)
-
-    @pl.when(step == pl.num_programs(0) - 1)
-    def _():
-        slots = slots_ref[...].astype(F32)
-        lane = lax.broadcasted_iota(jnp.int32, (1, TILE), 1)
-        live = lane < count_ref[0, 0]
-        tile_row = jnp.floor(slots * (1.0 / 32.0))
-        tile_col = slots - 32.0 * tile_row
-        tile_number = lax.broadcasted_iota(jnp.int32, (32, TILE), 0).astype(F32)
-        row_select = jnp.where(live & (tile_row == tile_number), 1.0, 0.0).astype(BF16)
-        col_select = jnp.where(live & (tile_col == tile_number), 1.0, 0.0).astype(BF16)
-        dst_ref[...] = jnp.dot(row_select, row_sums[...].astype(BF16), preferred_element_type=F32)
-        src_ref[...] = jnp.dot(col_select, col_sums[...].astype(BF16), preferred_element_type=F32)
-        info_ref[...] = jnp.zeros_like(info_ref)
-        for base, by_row in ((0, True), (4, False)):
-            for place, line in enumerate(sort_table(slots, live, by_row)):
-                info_ref[base + place : base + place + 1, :] = line
-
-
-def block_degrees(adj_tiles, slots, count):
-    slot_total = adj_tiles.shape[0]
-    return pl.pallas_call(
-        degree_kernel,
-        grid=(slot_total // CHUNK,),
-        in_specs=[
-            pl.BlockSpec(memory_space=pltpu.SMEM),
-            pl.BlockSpec((1, TILE), lambda i: (0, 0)),
-            pl.BlockSpec((CHUNK, TILE, TILE), lambda i: (i, 0, 0)),
-        ],
-        out_specs=[
-            pl.BlockSpec((CHUNK, TILE, TILE), lambda i: (i, 0, 0)),
-            pl.BlockSpec((32, TILE), lambda i: (0, 0)),
-            pl.BlockSpec((32, TILE), lambda i: (0, 0)),
-            pl.BlockSpec((8, TILE), lambda i: (0, 0)),
-        ],
-        out_shape=[
-            jax.ShapeDtypeStruct((slot_total, TILE, TILE), BF16),
-            jax.ShapeDtypeStruct((32, TILE), F32),
-            jax.ShapeDtypeStruct((32, TILE), F32),
-            jax.ShapeDtypeStruct((8, TILE), jnp.int32),
-        ],
-        scratch_shapes=[pltpu.VMEM((TILE, TILE), F32), pltpu.VMEM((TILE, TILE), F32)],
-        name="block_degrees",
-    )(count, slots, adj_tiles)
 
 
 def product_kernel(dims, count_ref, info_ref, tiles_ref, pair_ref, out_ref):
@@ -165,42 +108,89 @@
         in_specs=[pl.BlockSpec(memory_space=pltpu.SMEM)] * 2 + [VMEM_SPEC] * 2,
         out_specs=VMEM_SPEC,
         out_shape=jax.ShapeDtypeStruct((32, TILE, TILE), F32),
+        compiler_params=pltpu.CompilerParams(vmem_limit_bytes=LIMIT),
         name=name,
     )(count, info, tiles, pairs)
 
 
-LINE = ((0, 0), (1, -1), (1, 1), (2, -1), (2, 1), (3, -1), (3, 1))
+OUTWARD = ((0, 1, 2, 3), (1, 0, 2, 3), (2, 1, 3, 0), (3, 2, 1, 0))
+INWARD = tuple(order[::-1] for order in OUTWARD)
+
+
+def in_order(orders, place, z):
+    low, high = lax.rem(z, 2), lax.div(z, 2)
+    v = [orders[k][place] for k in range(4)]
+    return v[0] + (v[1] - v[0]) * low + (v[2] - v[0]) * high + (v[3] - v[2] - v[1] + v[0]) * low * high
 
 
 def gather_kernel(
-    feat_ref, src_ref, dst_ref, pair_ref, src_scale_ref, dst_scale_ref,
-    held, deg_sent, deg_got, recv_sem, z_sem, y_sem, relay_sem, deg_send_sem, deg_recv_sem,
+    count_ref, slots_ref, feat_ref, adj_ref,
+    tiles_ref, pair_ref, src_scale_ref, dst_scale_ref, forward_info_ref, backward_info_ref,
+    adj_got, row_sums, col_sums, parts, held, deg_sent, deg_got,
+    feat_sem, adj_sem, recv_sem, z_sem, y_sem, relay_sem, deg_send_sem, deg_recv_sem,
 ):
+    chunks = adj_ref.shape[0] // CHUNK
     row, col = lax.axis_index("row"), lax.axis_index("col")
     y, z = lax.div(row, 4), lax.rem(row, 4)
     y_up, y_down, y_far = lax.rem(y + 1, 4), lax.rem(y + 3, 4), lax.rem(y + 2, 4)
-    greet(
+    wait_for_all = greet(
         [lax.rem(y + d, 4) * 4 + z for d in (1, 2, 3)] + [y * 4 + lax.rem(z + d, 4) for d in (1, 2, 3)],
         [xor_peer(col, bit) for bit in (1, 2, 4, 8)],
     )
 
-    def own(z_from, half):
-        if z_from is None:
-            return feat_ref.at[half]
-        return held.at[y * 4 + z_from, half]
-
-    def z_copy(z_from, first, way, half):
+    def adj_copy(chunk):
+        here = pl.ds(pl.multiple_of(chunk * CHUNK, CHUNK), CHUNK)
+        return pltpu.make_async_copy(adj_ref.at[here], adj_got.at[here], adj_sem.at[chunk])
+
+    feat_copy = pltpu.make_async_copy(feat_ref, held.at[row], feat_sem)
+    feat_copy.start()
+    for chunk in range(chunks):
+        adj_copy(chunk).start()
+
+    ones = jnp.ones((TILE, TILE), F32).astype(BF16)
+    diagonal = lax.broadcasted_iota(jnp.int32, (TILE, TILE), 0) == lax.broadcasted_iota(
+        jnp.int32, (TILE, TILE), 1
+    )
+
+    def degree_chunks(first, last):
+        def body(chunk, carry):
+            adj_copy(chunk).wait()
+            for k in range(CHUNK):
+                slot = chunk * CHUNK + k
+                tile = adj_got[slot].astype(F32)
+                narrow = tile.astype(BF16)
+                tiles_ref[slot] = narrow
+                col_sums[pl.ds(slot, 1), :] = jnp.sum(tile, axis=0, keepdims=True)
+                sums = jnp.dot(narrow, ones, preferred_element_type=F32)
+                row_sums[pl.ds(slot, 1), :] = jnp.sum(jnp.where(diagonal, sums, 0.0), axis=0, keepdims=True)
+            return carry
+
+        lax.fori_loop(first, last, body, 0)
+
+    slots = slots_ref[...].astype(F32)
+    live = lax.broadcasted_iota(jnp.int32, (1, TILE), 1) < count_ref[0, 0]
+
+    def degree_parts():
+        tile_row = jnp.floor(slots * (1.0 / 32.0))
+        tile_col = slots - 32.0 * tile_row
+        tile_number = lax.broadcasted_iota(jnp.int32, (32, TILE), 0).astype(F32)
+        row_select = jnp.where(live & (tile_row == tile_number), 1.0, 0.0).astype(BF16)
+        col_select = jnp.where(live & (tile_col == tile_number), 1.0, 0.0).astype(BF16)
+        parts[0] = jnp.dot(col_select, col_sums[...].astype(BF16), preferred_element_type=F32)
+        parts[1] = jnp.dot(row_select, row_sums[...].astype(BF16), preferred_element_type=F32)
+
+    def z_copy(z_from, way, half):
         block = y * 4 + z_from
         return remote(
-            own(None if first else z_from, half), held.at[block, half],
+            held.at[block, half], held.at[block, half],
             z_sem.at[z_from, way, half], recv_sem.at[block, half],
             row=y * 4 + lax.rem(z + (1 if way == 0 else 3), 4),
         )
 
-    def y_copy(z_from, first, way, half):
+    def y_copy(z_from, way, half):
         block = y * 4 + z_from
         return remote(
-            own(None if first else z_from, half), held.at[block, half],
+            held.at[block, half], held.at[block, half],
             y_sem.at[z_from, way, half], recv_sem.at[block, half],
             row=(y_up if way == 0 else y_down) * 4 + z,
         )
@@ -219,67 +209,74 @@
             row=y_up * 4 + z,
         ).wait_recv()
 
-    def here(distance, sign):
-        return (z + sign * distance >= 0) & (z + sign * distance <= 3)
-
-    def on_way(distance, sign, action):
-        z_from = z + sign * distance
-        for way, goes in ((0, z < 3), (1, z > 0)):
-            if distance and (way == 0) != (sign < 0):
-                continue
+    def on_line(place, action):
+        z_from = in_order(OUTWARD, place, z)
+        for way in (0, 1):
+            goes = z < 3 if way == 0 else z > 0
+            if place:
+                goes = goes & (z_from < z if way == 0 else z_from > z)
 
             @pl.when(goes)
             def _():
                 for half in (0, 1):
-                    action(z_copy(z_from, distance == 0, way, half))
-
-    def column_step(distance, sign):
-        z_from = z + sign * distance
-        if distance:
+                    action(z_copy(z_from, way, half))
+
+    def column_step(place):
+        z_from = in_order(OUTWARD, place, z)
+        if place:
             for half in (0, 1):
                 arrived(y * 4 + z_from, half)
-        for half in (0, 1):
-            for way in (0, 1):
-                y_copy(z_from, distance == 0, way, half).start()
-        on_way(distance, sign, lambda copy: copy.start())
-
-    def relay_step(distance, sign):
-        z_from = z + sign * distance
+        on_line(place, lambda copy: copy.start())
+        for way, half in BY_WAY:
+            y_copy(z_from, way, half).start()
+
+    def relay_step(place):
+        z_from = in_order(OUTWARD, place, z)
         for half in (0, 1):
             arrived((y_down if half == 0 else y_up) * 4 + z_from, half)
             relay_copy(z_from, half).start()
 
+    def degree_source(which, step):
+        return parts.at[which] if step == 0 else deg_sent.at[which, step - 1]
+
     def degree_copy(which, step):
-        source = (src_ref, dst_ref)[which] if step == 0 else deg_sent.at[which, step - 1]
         where = {("row", "col")[which]: xor_peer((row, col)[which], 1 << step)}
         return remote(
-            source, deg_got.at[which, step], deg_send_sem.at[which, step], deg_recv_sem.at[which, step], **where
+            degree_source(which, step), deg_got.at[which, step],
+            deg_send_sem.at[which, step], deg_recv_sem.at[which, step], **where
         )
 
     def degree_step(step):
         for which in (0, 1):
-            copy = degree_copy(which, step)
-            copy.wait_recv()
-            source = (src_ref, dst_ref)[which] if step == 0 else deg_sent.at[which, step - 1]
-            deg_sent[which, step] = source[...] + deg_got[which, step]
+            degree_copy(which, step).wait_recv()
+            deg_sent[which, step] = degree_source(which, step)[...] + deg_got[which, step]
             if step < 3:
                 degree_copy(which, step + 1).start()
 
+    degree_chunks(0, chunks // 2)
+    feat_copy.wait()
+    wait_for_all()
+    column_step(0)
+    degree_chunks(chunks // 2, chunks)
+    degree_parts()
     for which in (0, 1):
         degree_copy(which, 0).start()
-    column_step(0, 0)
-    held[row] = feat_ref[...]
+    relay_step(0)
+    column_step(1)
     degree_step(0)
-    for place, (distance, sign) in enumerate(LINE[1:]):
-        pl.when(here(distance, sign))(functools.partial(column_step, distance, sign))
-        before = LINE[place]
-        pl.when(here(*before))(functools.partial(relay_step, *before))
-        if place in (1, 3, 5):
-            degree_step(1 + place // 2)
-    pl.when(here(*LINE[-1]))(functools.partial(relay_step, *LINE[-1]))
-
-    src_scale = lax.rsqrt(1.0 + deg_sent[0, 3])
-    src_scale_ref[...] = src_scale
+    relay_step(1)
+    column_step(2)
+    degree_step(1)
+    relay_step(2)
+    column_step(3)
+    degree_step(2)
+    for info_ref, by_row in ((forward_info_ref, True), (backward_info_ref, False)):
+        for place, line in enumerate(sort_table(slots, live, by_row)):
+            info_ref[place : place + 1, :] = line
+    relay_step(3)
+    degree_step(3)
+
+    src_scale_ref[...] = lax.rsqrt(1.0 + deg_sent[0, 3])
     dst_scale_ref[...] = lax.rsqrt(1.0 + deg_sent[1, 3])
 
     def settle(block):
@@ -288,53 +285,61 @@
             scale = to_column(src_scale_ref[pl.ds(tile, 1), :])
             pair_ref[tile] = split_pair(held[block, half] * scale)
 
-    for z_from in range(4):
-        settle(y * 4 + z_from)
-
-    def last_step(distance, sign):
-        z_from = z + sign * distance
+    for place in range(4):
+        settle(y * 4 + in_order(OUTWARD, place, z))
+    for place in range(4):
+        z_from = in_order(OUTWARD, place, z)
         arrived(y_down * 4 + z_from, 1)
         settle(y_down * 4 + z_from)
         arrived(y_up * 4 + z_from, 0)
         settle(y_up * 4 + z_from)
-
-    def far_step(distance, sign):
-        z_from = z + sign * distance
+    for place in range(4):
+        z_from = in_order(OUTWARD, place, z)
         arrived(y_far * 4 + z_from, 0)
         arrived(y_far * 4 + z_from, 1)
         settle(y_far * 4 + z_from)
-
-    def send_step(distance, sign):
-        z_from = z + sign * distance
+    for place in range(4):
+        z_from = in_order(OUTWARD, place, z)
         for half in (0, 1):
             for way in (0, 1):
-                y_copy(z_from, distance == 0, way, half).wait_send()
+                y_copy(z_from, way, half).wait_send()
             relay_copy(z_from, half).wait_send()
-        on_way(distance, sign, lambda copy: copy.wait_send())
-
-    for action in (last_step, far_step, send_step):
-        for item in LINE:
-            pl.when(here(*item))(functools.partial(action, *item))
+        on_line(place, lambda copy: copy.wait_send())
     for which in (0, 1):
         for step in range(4):
             degree_copy(which, step).wait_send()
 
 
-def gather_features(features, src_part, dst_part):
+def gather_features(features, adj_tiles, slots, count):
     dma = pltpu.SemaphoreType.DMA
+    slot_total = adj_tiles.shape[0]
     return pl.pallas_call(
         gather_kernel,
-        in_specs=[VMEM_SPEC] * 3,
-        out_specs=[VMEM_SPEC] * 3,
+        in_specs=[
+            pl.BlockSpec(memory_space=pltpu.SMEM),
+            VMEM_SPEC,
+            pl.BlockSpec(memory_space=pltpu.HBM),
+            pl.BlockSpec(memory_space=pltpu.HBM),
+        ],
+        out_specs=[VMEM_SPEC] * 6,
         out_shape=[
+            jax.ShapeDtypeStruct((slot_total, TILE, TILE), BF16),
             jax.ShapeDtypeStruct((32, TILE, 2 * TILE), BF16),
             jax.ShapeDtypeStruct((32, TILE), F32),
             jax.ShapeDtypeStruct((32, TILE), F32),
+            jax.ShapeDtypeStruct((3, TILE), jnp.int32),
+            jax.ShapeDtypeStruct((3, TILE), jnp.int32),
         ],
         scratch_shapes=[
+            pltpu.VMEM((slot_total, TILE, TILE), jnp.int32),
+            pltpu.VMEM((slot_total, TILE), F32),
+            pltpu.VMEM((slot_total, TILE), F32),
+            pltpu.VMEM((2, 32, TILE), F32),
             pltpu.VMEM((16, 2, TILE, TILE), F32),
             pltpu.VMEM((2, 4, 32, TILE), F32),
             pltpu.VMEM((2, 4, 32, TILE), F32),
+            dma,
+            dma((slot_total // CHUNK,)),
             dma((16, 2)),
             dma((4, 2, 2)),
             dma((4, 2, 2)),
@@ -342,9 +347,14 @@
             dma((2, 4)),
             dma((2, 4)),
         ],
-        compiler_params=pltpu.CompilerParams(collective_id=0, has_side_effects=True),
+        compiler_params=pltpu.CompilerParams(vmem_limit_bytes=LIMIT, collective_id=0, has_side_effects=True),
         name="gather_features",
-    )(features.reshape(2, TILE, TILE), src_part, dst_part)
+    )(
+        count,
+        slots,
+        pltpu.with_memory_space_constraint(features.reshape(2, TILE, TILE), pltpu.HBM),
+        pltpu.with_memory_space_constraint(adj_tiles, pltpu.HBM),
+    )
 
 
 WROWS = 72
@@ -362,7 +372,7 @@
     sibling = col + 1 - 2 * core
     z_peer = col + 2 - 4 * zh
     up, down = x_up * 4 + zh * 2 + core, x_down * 4 + zh * 2 + core
-    greet([], [sibling, z_peer, up, down, x_far * 4 + zh * 2 + core])
+    greet([], [sibling, z_peer, up, down, x_far * 4 + zh * 2 + core])()
 
     def sib_copy(place, which):
         target = (x_far, x_up, x_down, x)[place]
@@ -403,7 +413,6 @@
         for way in (0, 1):
             join(1 + way, which)
             near_copy(which, way, 1 - way).start()
-    for which in (0, 1):
         for way in (0, 1):
             far_copy(which, way).wait_recv()
             sib_got[1 + way, which, way] += (ring_a, ring_b)[way][which]
@@ -477,9 +486,8 @@
 
     for half in (0, 1):
         spread_z(half).start()
-    for half in (0, 1):
-        for way in (0, 1):
-            spread_x(0, way, half).start()
+    for way, half in BY_WAY:
+        spread_x(0, way, half).start()
     for half in (0, 1):
         spread_sib(0, 0, half).start()
 
@@ -608,14 +616,14 @@
             dma((4, 2)), dma((4, 2)), dma((2, 2)), dma((2, 2)), dma((2, 2, 2)), dma((2, 2, 2)), dma((2,)), dma((2,)),
             dma((16, 2)), dma((2,)), dma((2, 2, 2)), dma((2, 2)), dma((4, 2, 2)), dma((4,)), dma((4,)),
         ],
-        compiler_params=pltpu.CompilerParams(collective_id=1, has_side_effects=True),
+        compiler_params=pltpu.CompilerParams(vmem_limit_bytes=LIMIT, collective_id=1, has_side_effects=True),
         name="dense_layer",
     )(part.reshape((16, 2) + half), weight, bias_vector.reshape(1, TILE), out_grad, dst_scale)
 
 
 def scatter_kernel(
-    part_ref, wsum_ref, scale_ref, grad_ref, wgrad_ref,
-    staged_a, staged_b, ring_a, ring_b, from_down, from_up, total, line_up, line_down, w_sent, w_got, w_all,
+    part_ref, wsum_ref, scale_ref, grad_ref, wgrad_ref, bgrad_ref,
+    staged_a, staged_b, ring_a, ring_b, from_down, from_up, total, line_up, line_down, w_sent, w_got, w_all, w_full,
     far_ssem, far_rsem, near_ssem, near_rsem, line_ssem, line_rsem, w_ssem, w_rsem,
 ):
     row, col = lax.axis_index("row"), lax.axis_index("col")
@@ -626,11 +634,8 @@
     greet(
         [lax.rem(y + d, 4) * 4 + z for d in (1, 2, 3)] + [y * 4 + lax.rem(z + d, 4) for d in (1, 2, 3)],
         [sibling],
-    )
+    )()
     up, down = y_up * 4 + z, y_down * 4 + z
-
-    def here(distance, sign):
-        return (z + sign * distance >= 0) & (z + sign * distance <= 3)
 
     def far_copy(zb, way):
         return remote(
@@ -664,73 +669,90 @@
         w_sent[step] = source[...] + w_got[step]
         w_copy(step + 1).start()
 
-    def open_step(distance, sign):
-        zb = z + sign * distance
-        for way in (0, 1):
-            far_copy(zb, way).start()
-        for way in (0, 1):
-            near_copy(zb, way, 1 - way).start()
-
-    def relay_step(distance, sign):
-        zb = z + sign * distance
+    zbs = [in_order(INWARD, place, z) for place in range(4)]
+
+    def far_step(place):
+        for way in (0, 1):
+            far_copy(zbs[place], way).start()
+
+    def near_step(place):
+        for way in (0, 1):
+            near_copy(zbs[place], way, 1 - way).start()
+
+    def relay_step(place):
+        zb = zbs[place]
         for way in (0, 1):
             far_copy(zb, way).wait_recv()
             block = (y_up, y_down)[way] * 4 + zb
             (staged_a, staged_b)[way][zb] = part_ref[block, way] + (ring_a, ring_b)[way][zb]
             near_copy(zb, way, way).start()
 
-    def close_step(distance, sign):
-        zb = z + sign * distance
-        for half in (0, 1):
+    def line_ways(place):
+        zb = zbs[place]
+        if place == 3:
+            return ((0, z > 0, None), (1, z < 3, None))
+        return ((0, (zb > z) & (z > 0), zb > z), (1, (zb < z) & (z < 3), zb < z))
+
+    def close_step(place):
+        zb = zbs[place]
+        for half in (1, 0):
             for way in (0, 1):
                 near_copy(zb, way, half).wait_recv()
             total[zb, half] = part_ref[y * 4 + zb, half] + from_down[zb, half] + from_up[zb, half]
-
-        def collect(way):
-            for half in (0, 1):
-                line_copy(zb, way, half).wait_recv()
-                total[zb, half] += (line_up, line_down)[way][zb, half]
-
-        if distance == 0:
-            pl.when(z > 0)(functools.partial(collect, 0))
-            pl.when(z < 3)(functools.partial(collect, 1))
-        else:
-            way = 0 if sign > 0 else 1
-            pl.when(z > 0 if way == 0 else z < 3)(functools.partial(collect, way))
-            for half in (0, 1):
-                line_copy(zb, way, half).start()
-
-    def send_step(distance, sign):
-        zb = z + sign * distance
+        for way, comes, goes in line_ways(place):
+            for half in (1, 0):
+
+                @pl.when(comes)
+                def _():
+                    line_copy(zb, way, half).wait_recv()
+                    total[zb, half] += (line_up, line_down)[way][zb, half]
+
+                if goes is not None:
+                    pl.when(goes)(lambda: line_copy(zb, way, half).start())
+
+    def send_step(place):
+        zb = zbs[place]
         for way in (0, 1):
             far_copy(zb, way).wait_send()
             for half in (0, 1):
                 near_copy(zb, way, half).wait_send()
-        if distance:
+        for way, _, goes in line_ways(place):
             for half in (0, 1):
-                line_copy(zb, 0 if sign > 0 else 1, half).wait_send()
-
-    backwards = LINE[::-1]
-    for item in backwards:
-        pl.when(here(*item))(functools.partial(open_step, *item))
+                if goes is not None:
+                    pl.when(goes)(lambda: line_copy(zb, way, half).wait_send())
+
+    far_step(0)
+    near_step(0)
+    far_step(1)
     w_copy(0).start()
-    for place, item in enumerate(backwards):
-        pl.when(here(*item))(functools.partial(relay_step, *item))
-        if place >= 1:
-            before = backwards[place - 1]
-            pl.when(here(*before))(functools.partial(close_step, *before))
-        if place in (2, 3, 4, 6):
-            w_step((2, 3, 4, 6).index(place))
-    close_step(*backwards[-1])
+    relay_step(0)
+    near_step(1)
+    far_step(2)
+    relay_step(1)
+    near_step(2)
+    far_step(3)
+    close_step(0)
+    relay_step(2)
+    near_step(3)
+    w_step(0)
+    close_step(1)
+    relay_step(3)
+    w_step(1)
+    close_step(2)
+    w_step(2)
+    w_step(3)
+    close_step(3)
 
     for half in (0, 1):
         scale = to_column(scale_ref[pl.ds(2 * row + half, 1), :])
         grad_ref[pl.ds(half * TILE, TILE), :] = total[z, half] * scale
     w_copy(4).wait_recv()
-    wgrad_ref[pl.ds(pl.multiple_of(core * WROWS, 8), WROWS), :] = w_sent[3]
-    wgrad_ref[pl.ds(pl.multiple_of((1 - core) * WROWS, 8), WROWS), :] = w_all[...]
-    for item in backwards:
-        pl.when(here(*item))(functools.partial(send_step, *item))
+    w_full[pl.ds(pl.multiple_of(core * WROWS, 8), WROWS), :] = w_sent[3]
+    w_full[pl.ds(pl.multiple_of((1 - core) * WROWS, 8), WROWS), :] = w_all[...]
+    wgrad_ref[...] = w_full[0:TILE, :]
+    bgrad_ref[...] = w_full[TILE : TILE + 1, :]
+    for place in range(4):
+        send_step(place)
     for step in range(5):
         w_copy(step).wait_send()
 
@@ -741,10 +763,11 @@
     return pl.pallas_call(
         scatter_kernel,
         in_specs=[VMEM_SPEC] * 3,
-        out_specs=[VMEM_SPEC] * 2,
+        out_specs=[VMEM_SPEC] * 3,
         out_shape=[
             jax.ShapeDtypeStruct((2 * TILE, TILE), F32),
-            jax.ShapeDtypeStruct((2 * WROWS, TILE), F32),
+            jax.ShapeDtypeStruct((TILE, TILE), F32),
+            jax.ShapeDtypeStruct((1, TILE), F32),
         ],
         scratch_shapes=[
             pltpu.VMEM((4,) + half, F32),
@@ -759,21 +782,23 @@
             pltpu.VMEM((4, WROWS, TILE), F32),
             pltpu.VMEM((4, WROWS, TILE), F32),
             pltpu.VMEM((WROWS, TILE), F32),
+            pltpu.VMEM((2 * WROWS, TILE), F32),
             dma((4, 2)), dma((4, 2)), dma((4, 2, 2)), dma((4, 2, 2)), dma((4, 2)), dma((4, 2, 2)), dma((5,)), dma((5,)),
         ],
-        compiler_params=pltpu.CompilerParams(collective_id=2, has_side_effects=True),
+        compiler_params=pltpu.CompilerParams(vmem_limit_bytes=LIMIT, collective_id=2, has_side_effects=True),
         name="scatter_gradients",
     )(part.reshape((16, 2) + half), wsum, src_scale)
 
 
 def local(features, weight, bias_vector, out_grad, adj_tiles, tile_slots, tile_counts):
-    tiles, dst_part, src_part, info = block_degrees(adj_tiles[0, 0], tile_slots[0], tile_counts)
-    pairs, src_scale, dst_scale = gather_features(features, src_part, dst_part)
-    part = sparse_product(NN, tile_counts, info[:4], tiles, pairs, "forward_product")
+    tiles, pairs, src_scale, dst_scale, forward_info, backward_info = gather_features(
+        features, adj_tiles[0, 0], tile_slots[0], tile_counts
+    )
+    part = sparse_product(NN, tile_counts, forward_info, tiles, pairs, "forward_product")
     activated, grad_pairs, wsum = dense_layer(part, weight, bias_vector, out_grad, dst_scale)
-    back = sparse_product(TN, tile_counts, info[4:], tiles, grad_pairs, "backward_product")
-    feature_grad, wgrad = scatter_gradients(back, wsum, src_scale)
-    return activated, feature_grad, wgrad[:TILE], wgrad[TILE]
+    back = sparse_product(TN, tile_counts, backward_info, tiles, grad_pairs, "backward_product")
+    feature_grad, weight_grad, bias_grad = scatter_gradients(back, wsum, src_scale)
+    return activated, feature_grad, weight_grad, bias_grad.reshape(TILE)
 
 
 def solution(mesh):

time: 152 us -> 117 us (0.77)
  the two profiles are of different devices: /device:TPU:2 before, /device:TPU:1 now
where the time goes in v2:
time: 117 us; the launch traced here: 118 us
  Pallas kernels  113 us (97%)
  local copies, waits for them, and re-layouts  3.12 us (3%)
  between operations  1.38 us (1%)
    pallas_call x1, Pallas kernels, dense_layer(): pl.pallas_call(layer_kernel, in_specs=[VMEM_SPEC] * 5, out_specs=[VMEM_SP...  44.4 us
    pallas_call x1, Pallas kernels, scatter_gradients(): pl.pallas_call(scatter_kernel, in_specs=[VMEM_SPEC] * 3, out_specs=[VMEM_...  34.2 us
    pallas_call x1, Pallas kernels, gather_features(): pl.pallas_call(gather_kernel, in_specs=[pl.BlockSpec(memory_space=pltpu.S...  31.1 us
    pallas_call x2, Pallas kernels, sparse_product(): pl.pallas_call(functools.partial(product_kernel, dims), in_specs=[pl.Bloc...  3.33 us
    unnamed x12, local copies, waits for them, and re-layouts  3.12 us

profile of v2, /device:TPU:1, one launch (start us, length us, event | category | flops | bytes accessed | tf_op | source)
XLA Modules:
  0.0 117.6 jit_solution(1029938859085780005)
XLA Ops:
  1.3 0.0 copy-start.2
  1.3 0.6 copy-done.2
  1.9 31.1 %gather_features.1 = (bf16[128,128,128]{2,1,0:T(8,128)(2,1)S(1)}, bf16[32,128,256]{2,1,0:T(8,128)(2,1)S(1)}, f32[32,128]{1,0:T(8,128)S(1)}, f32[32,128]{1,0:T(8,...) custom-call(s32[1,1]{1,0:T(1,128)S(6)} %copy.15.count_ref, s32[1,128]{1,0:T(1,128)S(1)} %bitcast.9, ...), custom_call_target="tpu_custom_call" | custom-call | tf_op jit(solution)/shard_map/gather_features/pallas_call | solution.py:316
  33.1 0.0 copy-start
  33.1 0.0 copy-start.1
  33.1 0.0 copy-start.3
  33.1 1.6 %forward_product.1 = f32[32,128,128]{2,1,0:T(8,128)S(1)} custom-call(s32[1,1]{1,0:T(1,128)S(6)} %copy.15.count_ref, s32[3,128]{1,0:T(4,128)S(1)} %get-tuple-element.16.info_ref, bf16[128,128,128]{2,1,0:T(8,128)(2,1)S(1)} %get-tuple-element.17.tiles_ref, bf16[32,128,256]{2,1,0:T(8,128)(2,1)S(1)} %get-tuple-element.18.pair_ref), custom_call_target="tpu_custom_call" | custom-call | tf_op jit(solution)/shard_map/forward_product/pallas_call | solution.py:106
  34.7 0.0 copy-done
  34.8 0.0 copy-done.1
  34.8 0.0 copy-done.3
  34.8 44.4 %dense_layer.1 = (f32[256,128]{1,0:T(8,128)S(1)}, bf16[32,128,256]{2,1,0:T(8,128)(2,1)S(1)}, f32[72,128]{1,0:T(8,128)S(1)}) custom-call(f32[16,2,128,128]{3,2,1,0:T(8,128)S(1)} %bitcast.7, f32[128,128]{1,0:T(8,128)S(1)} %copy-done.1, f32[1,128]{1,0:T(1,128)S(1)} %bitcast.10, f32[256,128]{1,0:T(8,128)S(1)} %copy-done, f32[32,128]{1,0:T(8,128)S(1)} %get-tuple-element.19.scale_ref), custom_call_target="tpu_custom_call" | custom-call | tf_op jit(solution)/shard_map/dense_layer/pallas_call | solution.py:595
  79.2 1.7 %backward_product.1 = f32[32,128,128]{2,1,0:T(8,128)S(1)} custom-call(s32[1,1]{1,0:T(1,128)S(6)} %copy.15.count_ref, s32[3,128]{1,0:T(4,128)S(1)} %get-tuple-element.21.info_ref, bf16[128,128,128]{2,1,0:T(8,128)(2,1)S(1)} %get-tuple-element.17.tiles_ref, bf16[32,128,256]{2,1,0:T(8,128)(2,1)S(1)} %get-tuple-element.22.pair_ref), custom_call_target="tpu_custom_call" | custom-call | tf_op jit(solution)/shard_map/backward_product/pallas_call | solution.py:106
  80.9 34.2 %scatter_gradients.1 = (f32[256,128]{1,0:T(8,128)S(1)}, f32[128,128]{1,0:T(8,128)S(1)}, f32[1,128]{1,0:T(1,128)S(1)}) custom-call(f32[16,2,128,128]{3,2,1,0:T(8,128)S(1)} %bitcast.8, f32[72,128]{1,0:T(8,128)S(1)} %get-tuple-element.23.wsum_ref, f32[32,128]{1,0:T(8,128)S(1)} %get-tuple-element.24.scale_ref), custom_call_target="tpu_custom_call" | custom-call | tf_op jit(solution)/shard_map/scatter_gradients/pallas_call | solution.py:763
  115.1 0.7 copy.16
  115.8 0.7 copy.17
  116.4 0.6 copy.18
  117.1 0.5 copy.19
Async XLA Ops:
  1.3 0.7 copy-start.2
  33.1 1.7 %copy-start = (f32[256,128]{1,0:T(8,128)S(1)}, f32[256,128]{1,0:T(8,128)}, u32[]{:S(2)}) copy-start(f32[256,128]{1,0:T(8,128)} %grad_ref.1) | copy-start | bytes 393220
  33.1 1.7 %copy-start.1 = (f32[128,128]{1,0:T(8,128)S(1)}, f32[128,128]{1,0:T(8,128)}, u32[]{:S(2)}) copy-start(f32[128,128]{1,0:T(8,128)} %w_ref.1) | copy-start | bytes 196612
  33.1 1.7 %copy-start.3 = (f32[128]{0:T(128)S(1)}, f32[128]{0:T(128)}, u32[]{:S(2)}) copy-start(f32[128]{0:T(128)} %param.9) | copy-start | bytes 1540

commit v3 on v2

v3 whole, which is shorter than its diff:
```python
import functools

import jax
import jax.numpy as jnp
from jax import lax
from jax.experimental import pallas as pl
from jax.experimental.pallas import tpu as pltpu
from jax.sharding import PartitionSpec as P

TILE = 128
MESH = pl.DeviceIdType.MESH
F32 = jnp.float32
BF16 = jnp.bfloat16
HIGHEST = lax.Precision.HIGHEST
VMEM_SPEC = pl.BlockSpec(memory_space=pltpu.VMEM)
CHUNK = 8
LIMIT = 24 << 20
GATHER_PIECES = 2
LAYER_PIECES = 2
SCATTER_PIECES = 2


def block_of(pieces):
    return (pieces, 2 * TILE // pieces, TILE)


def by_way(pieces):
    return [(piece % 2, piece) for piece in range(pieces)] + [(piece % 2, piece + 1 - 2 * (piece % 2)) for piece in range(pieces)]


def piece_columns(scale_ref, first, pieces):
    columns = [to_column(scale_ref[pl.ds(first + half, 1), :]) for half in (0, 1)]
    each = pieces // 2
    rows = TILE // each
    return [columns[k // each][k % each * rows : (k % each + 1) * rows] for k in range(pieces)]
NT = (((1,), (1,)), ((), ()))
NN = (((1,), (0,)), ((), ()))
TN = (((0,), (0,)), ((), ()))


def remote(src, dst, send_sem, recv_sem, **where):
    return pltpu.make_async_remote_copy(
        src_ref=src,
        dst_ref=dst,
        send_sem=send_sem,
        recv_sem=recv_sem,
        device_id=where,
        device_id_type=MESH,
    )


def xor_peer(index, bit):
    return index + bit - 2 * bit * lax.rem(lax.div(index, bit), 2)


def greet(rows, cols):
    barrier = pltpu.get_barrier_semaphore()
    for peer in rows:
        pl.semaphore_signal(barrier, inc=1, device_id={"row": peer}, device_id_type=MESH)
    for peer in cols:
        pl.semaphore_signal(barrier, inc=1, device_id={"col": peer}, device_id_type=MESH)
    return lambda: pl.semaphore_wait(barrier, len(rows) + len(cols))


def to_column(row_vector):
    spread = jnp.broadcast_to(row_vector, (TILE, TILE))
    diagonal = lax.broadcasted_iota(jnp.int32, (TILE, TILE), 0) == lax.broadcasted_iota(
        jnp.int32, (TILE, TILE), 1
    )
    return jnp.sum(jnp.where(diagonal, spread, 0.0), axis=1, keepdims=True)


def split_pair(value):
    high = value.astype(BF16)
    low = (value - high.astype(F32)).astype(BF16)
    return jnp.concatenate([high, low], axis=1)


def put_pair(pair_ref, block, piece, pieces, value):
    each = pieces // 2
    rows = TILE // each
    here = slice(piece % each * rows, (piece % each + 1) * rows)
    pair_ref[2 * block + piece // each, here, :] = split_pair(value)


def sort_table(slots, live, by_row):
    tile_row = jnp.floor(slots * (1.0 / 32.0))
    tile_col = slots - 32.0 * tile_row
    lane = lax.broadcasted_iota(jnp.int32, (1, TILE), 1).astype(F32)
    key = jnp.where(live, tile_row * 32.0 + tile_col if by_row else tile_col * 32.0 + tile_row, 2048.0 + lane)
    key_column = to_column(key)
    rank = jnp.sum(jnp.where(key < key_column, 1.0, 0.0), axis=1, keepdims=True)
    place = rank == lax.broadcasted_iota(jnp.int32, (TILE, TILE), 1).astype(F32)
    number = lax.broadcasted_iota(jnp.int32, (TILE, 1), 0).astype(F32)

    def moved(column):
        return jnp.sum(jnp.where(place, column, 0.0), axis=0, keepdims=True).astype(jnp.int32)

    ends = (to_column(tile_row), to_column(tile_col))
    if not by_row:
        ends = ends[::-1]
    live_column = to_column(jnp.where(live, 1.0, 0.0))
    target = lax.broadcasted_iota(jnp.int32, (TILE, TILE), 1).astype(F32)

    def counted(which):
        return jnp.sum(jnp.where(which, live_column, 0.0), axis=0, keepdims=True).astype(jnp.int32)

    return moved(number), moved(ends[0]), moved(ends[1]), counted(ends[0] < target), counted(ends[0] <= target)


def block_product(dims, count_ref, info_ref, tiles_ref, pair_ref, sums_ref, first, last, total):
    unroll = 8
    count = count_ref[0, 0]

    def body(step, total):
        for u in range(unroll):
            k = step * unroll + u
            at = jnp.clip(count - 1, 0, k)
            number = jnp.clip(info_ref[0, at], 0, tiles_ref.shape[0] - 1)
            source = jnp.clip(info_ref[2, at], 0, pair_ref.shape[0] - 1)
            both = lax.dot_general(tiles_ref[number], pair_ref[source], dims, preferred_element_type=F32)
            goes_on = (k > 0) & (info_ref[1, jnp.maximum(at - 1, 0)] == info_ref[1, at])
            total = both[:, :TILE] + both[:, TILE:] + jnp.where(goes_on, total, 0.0)
            sums_ref[k] = total
        return total

    return lax.fori_loop(first, last, body, total)


def take_block(info_ref, sums_ref, part_ref, block):
    rows = part_ref.shape[2]
    each = TILE // rows
    for half in (0, 1):
        first, end = info_ref[3, 2 * block + half], info_ref[4, 2 * block + half]
        tile = jnp.where(end > first, sums_ref[jnp.clip(end - 1, 0, sums_ref.shape[0] - 1)], 0.0)
        for k in range(each):
            part_ref[block, half * each + k] = tile[k * rows : (k + 1) * rows]


def split_rows(value, order):
    high = value.astype(BF16)
    low = (value - high.astype(F32)).astype(BF16)
    return jnp.concatenate([(high, low)[k] for k in order], axis=0)


def split_columns(value):
    high = value.astype(BF16)
    low = (value - high.astype(F32)).astype(BF16)
    return jnp.concatenate([high, low, high], axis=1)


OUTWARD = ((0, 1, 2, 3), (1, 0, 2, 3), (2, 1, 3, 0), (3, 2, 1, 0))
INWARD = tuple(order[::-1] for order in OUTWARD)


def in_order(orders, place, z):
    low, high = lax.rem(z, 2), lax.div(z, 2)
    v = [orders[k][place] for k in range(4)]
    return v[0] + (v[1] - v[0]) * low + (v[2] - v[0]) * high + (v[3] - v[2] - v[1] + v[0]) * low * high


def gather_kernel(
    count_ref, slots_ref, feat_ref, adj_ref,
    tiles_ref, pair_ref, src_scale_ref, dst_scale_ref, forward_info_ref, backward_info_ref,
    adj_got, row_sums, col_sums, parts, held, slots_got, deg_sent, deg_got,
    feat_sem, adj_sem, recv_sem, z_sem, y_sem, relay_sem, deg_send_sem, deg_recv_sem,
):
    chunks = adj_ref.shape[0] // CHUNK
    row, col = lax.axis_index("row"), lax.axis_index("col")
    y, z = lax.div(row, 4), lax.rem(row, 4)
    y_up, y_down, y_far = lax.rem(y + 1, 4), lax.rem(y + 3, 4), lax.rem(y + 2, 4)
    wait_for_all = greet(
        [lax.rem(y + d, 4) * 4 + z for d in (1, 2, 3)] + [y * 4 + lax.rem(z + d, 4) for d in (1, 2, 3)],
        [xor_peer(col, bit) for bit in (1, 2, 4, 8)],
    )

    def adj_copy(chunk):
        here = pl.ds(pl.multiple_of(chunk * CHUNK, CHUNK), CHUNK)
        return pltpu.make_async_copy(adj_ref.at[here], adj_got.at[here], adj_sem.at[chunk])

    feat_copy = pltpu.make_async_copy(feat_ref, held.at[row], feat_sem.at[0])
    feat_copy.start()
    slots_copy = pltpu.make_async_copy(slots_ref, slots_got, feat_sem.at[1])
    slots_copy.start()
    for chunk in range(chunks):
        adj_copy(chunk).start()

    ones = jnp.ones((TILE, TILE), F32).astype(BF16)
    diagonal = lax.broadcasted_iota(jnp.int32, (TILE, TILE), 0) == lax.broadcasted_iota(
        jnp.int32, (TILE, TILE), 1
    )

    def degree_chunks(first, last):
        def body(chunk, carry):
            adj_copy(chunk).wait()
            for k in range(CHUNK):
                slot = chunk * CHUNK + k
                tile = adj_got[slot].astype(F32)
                narrow = tile.astype(BF16)
                tiles_ref[slot] = narrow
                col_sums[pl.ds(slot, 1), :] = jnp.sum(tile, axis=0, keepdims=True)
                sums = jnp.dot(narrow, ones, preferred_element_type=F32)
                row_sums[pl.ds(slot, 1), :] = jnp.sum(jnp.where(diagonal, sums, 0.0), axis=0, keepdims=True)
            return carry

        lax.fori_loop(first, last, body, 0)

    slots_copy.wait()
    slots = slots_got[...].astype(F32)
    live = lax.broadcasted_iota(jnp.int32, (1, TILE), 1) < count_ref[0, 0]

    def degree_parts():
        tile_row = jnp.floor(slots * (1.0 / 32.0))
        tile_col = slots - 32.0 * tile_row
        tile_number = lax.broadcasted_iota(jnp.int32, (32, TILE), 0).astype(F32)
        row_select = jnp.where(live & (tile_row == tile_number), 1.0, 0.0).astype(BF16)
        col_select = jnp.where(live & (tile_col == tile_number), 1.0, 0.0).astype(BF16)
        parts[0] = jnp.dot(col_select, col_sums[...].astype(BF16), preferred_element_type=F32)
        parts[1] = jnp.dot(row_select, row_sums[...].astype(BF16), preferred_element_type=F32)

    def z_copy(z_from, way, piece):
        block = y * 4 + z_from
        return remote(
            held.at[block, piece], held.at[block, piece],
            z_sem.at[z_from, way, piece], recv_sem.at[block, piece],
            row=y * 4 + lax.rem(z + (1 if way == 0 else 3), 4),
        )

    def y_copy(z_from, way, piece):
        block = y * 4 + z_from
        return remote(
            held.at[block, piece], held.at[block, piece],
            y_sem.at[z_from, way, piece], recv_sem.at[block, piece],
            row=(y_up, y_down)[way] * 4 + z,
        )

    def relay_copy(z_from, piece):
        way = piece % 2
        block = (y_down, y_up)[way] * 4 + z_from
        return remote(
            held.at[block, piece], held.at[block, piece],
            relay_sem.at[z_from, piece], recv_sem.at[block, piece],
            row=(y_up, y_down)[way] * 4 + z,
        )

    def arrived(block, piece):
        remote(
            held.at[block, piece], held.at[block, piece], relay_sem.at[0, piece], recv_sem.at[block, piece],
            row=y_up * 4 + z,
        ).wait_recv()

    def on_line(place, pieces, action):
        z_from = in_order(OUTWARD, place, z)
        for way in (0, 1):
            goes = z < 3 if way == 0 else z > 0
            if place:
                goes = goes & (z_from < z if way == 0 else z_from > z)

            @pl.when(goes)
            def _():
                for piece in pieces:
                    action(z_copy(z_from, way, piece))

    def column_step(place):
        z_from = in_order(OUTWARD, place, z)
        if place:
            for piece in range(GATHER_PIECES):
                arrived(y * 4 + z_from, piece)
        on_line(place, range(GATHER_PIECES), lambda copy: copy.start())
        for way, piece in by_way(GATHER_PIECES):
            y_copy(z_from, way, piece).start()

    def relay_step(place):
        z_from = in_order(OUTWARD, place, z)
        for piece in range(GATHER_PIECES):
            arrived((y_down, y_up)[piece % 2] * 4 + z_from, piece)
            relay_copy(z_from, piece).start()

    def degree_source(which, step):
        return parts.at[which] if step == 0 else deg_sent.at[which, step - 1]

    def degree_copy(which, step):
        where = {("row", "col")[which]: xor_peer((row, col)[which], 1 << step)}
        return remote(
            degree_source(which, step), deg_got.at[which, step],
            deg_send_sem.at[which, step], deg_recv_sem.at[which, step], **where
        )

    def degree_step(step):
        for which in (0, 1):
            degree_copy(which, step).wait_recv()
            deg_sent[which, step] = degree_source(which, step)[...] + deg_got[which, step]
            if step < 3:
                degree_copy(which, step + 1).start()

    degree_chunks(0, chunks // 4)
    feat_copy.wait()
    wait_for_all()
    column_step(0)
    degree_chunks(chunks // 4, chunks // 2 + 2)
    relay_step(0)
    column_step(1)
    degree_chunks(chunks // 2 + 2, chunks)
    degree_parts()
    for which in (0, 1):
        degree_copy(which, 0).start()
    relay_step(1)
    column_step(2)
    degree_step(0)
    relay_step(2)
    degree_step(1)
    column_step(3)
    degree_step(2)
    for info_ref, by_row in ((forward_info_ref, True), (backward_info_ref, False)):
        for place, line in enumerate(sort_table(slots, live, by_row)):
            info_ref[place : place + 1, :] = line
    relay_step(3)
    degree_step(3)

    src_scale_ref[...] = lax.rsqrt(1.0 + deg_sent[0, 3])
    dst_scale_ref[...] = lax.rsqrt(1.0 + deg_sent[1, 3])

    def settle(block):
        for piece, scale in enumerate(piece_columns(src_scale_ref, 2 * block, GATHER_PIECES)):
            put_pair(pair_ref, block, piece, GATHER_PIECES, held[block, piece] * scale)

    for place in range(4):
        settle(y * 4 + in_order(OUTWARD, place, z))
    for place in range(4):
        z_from = in_order(OUTWARD, place, z)
        for way in (0, 1):
            block = (y_down, y_up)[way] * 4 + z_from
            for piece in range(1 - way, GATHER_PIECES, 2):
                arrived(block, piece)
            settle(block)
    for place in range(4):
        z_from = in_order(OUTWARD, place, z)
        for piece in range(GATHER_PIECES):
            arrived(y_far * 4 + z_from, piece)
        settle(y_far * 4 + z_from)
    for place in range(4):
        z_from = in_order(OUTWARD, place, z)
        for piece in range(GATHER_PIECES):
            for way in (0, 1):
                y_copy(z_from, way, piece).wait_send()
            relay_copy(z_from, piece).wait_send()
        on_line(place, range(GATHER_PIECES), lambda copy: copy.wait_send())
    for which in (0, 1):
        for step in range(4):
            degree_copy(which, step).wait_send()


def gather_features(features, adj_tiles, slots, count):
    dma = pltpu.SemaphoreType.DMA
    slot_total = adj_tiles.shape[0]
    return pl.pallas_call(
        gather_kernel,
        in_specs=[
            pl.BlockSpec(memory_space=pltpu.SMEM),
            pl.BlockSpec(memory_space=pltpu.HBM),
            pl.BlockSpec(memory_space=pltpu.HBM),
            pl.BlockSpec(memory_space=pltpu.HBM),
        ],
        out_specs=[VMEM_SPEC] * 6,
        out_shape=[
            jax.ShapeDtypeStruct((slot_total, TILE, TILE), BF16),
            jax.ShapeDtypeStruct((32, TILE, 2 * TILE), BF16),
            jax.ShapeDtypeStruct((32, TILE), F32),
            jax.ShapeDtypeStruct((32, TILE), F32),
            jax.ShapeDtypeStruct((5, TILE), jnp.int32),
            jax.ShapeDtypeStruct((5, TILE), jnp.int32),
        ],
        scratch_shapes=[
            pltpu.VMEM((slot_total, TILE, TILE), jnp.int32),
            pltpu.VMEM((slot_total, TILE), F32),
            pltpu.VMEM((slot_total, TILE), F32),
            pltpu.VMEM((2, 32, TILE), F32),
            pltpu.VMEM((16,) + block_of(GATHER_PIECES), F32),
            pltpu.VMEM((1, TILE), jnp.int32),
            pltpu.VMEM((2, 4, 32, TILE), F32),
            pltpu.VMEM((2, 4, 32, TILE), F32),
            dma((2,)),
            dma((slot_total // CHUNK,)),
            dma((16, GATHER_PIECES)),
            dma((4, 2, GATHER_PIECES)),
            dma((4, 2, GATHER_PIECES)),
            dma((4, GATHER_PIECES)),
            dma((2, 4)),
            dma((2, 4)),
        ],
        compiler_params=pltpu.CompilerParams(vmem_limit_bytes=LIMIT, collective_id=0, has_side_effects=True),
        name="gather_features",
    )(
        count,
        pltpu.with_memory_space_constraint(slots, pltpu.HBM),
        pltpu.with_memory_space_constraint(features.reshape(block_of(GATHER_PIECES)), pltpu.HBM),
        pltpu.with_memory_space_constraint(adj_tiles, pltpu.HBM),
    )


SLICE = (16, TILE)


def layer_kernel(
    count_ref, info_ref, tiles_ref, source_ref, w_ref, b_ref, grad_ref, scale_ref, act_ref, pair_ref, wsum_ref,
    sums, part_ref, w_fore, w_back, sib_got, ring, from_left, from_right, z_sent, z_got, held, aggs, grads, wgrad, w_got,
    sib_ssem, sib_rsem, far_ssem, far_rsem, near_ssem, near_rsem, z_ssem, z_rsem,
    recv_sem, zg_sem, xg_sem, relay_sem, sg_sem, w_ssem, w_rsem,
):
    col = lax.axis_index("col")
    x, zh, core = lax.div(col, 4), lax.rem(lax.div(col, 2), 2), lax.rem(col, 2)
    x_up, x_down, x_far = lax.rem(x + 1, 4), lax.rem(x + 3, 4), lax.rem(x + 2, 4)
    sibling = col + 1 - 2 * core
    z_peer = col + 2 - 4 * zh
    up, down = x_up * 4 + zh * 2 + core, x_down * 4 + zh * 2 + core
    wait_for_all = greet([], [lax.rem(col + d, 16) for d in range(1, 16)])
    block_product(
        NN, count_ref, info_ref, tiles_ref, source_ref, sums, 0, tiles_ref.shape[0] // 8, jnp.zeros((TILE, TILE), F32)
    )
    w_fore[...] = split_rows(w_ref[...], (0, 0, 1))
    w_back[...] = split_rows(jnp.transpose(w_ref[...]), (0, 0, 1))
    first, rest = (0, 1), range(2, LAYER_PIECES)
    after = [(piece % 2, piece + 1 - 2 * (piece % 2)) for piece in rest]

    def sib_copy(place, which):
        target = (x_far, x_up, x_down, x)[place]
        half_z = 1 - zh if which == 0 else zh
        return remote(
            part_ref.at[target * 4 + half_z * 2 + 1 - core], sib_got.at[place, which],
            sib_ssem.at[place, which], sib_rsem.at[place, which], col=sibling,
        )

    def far_copy(which, piece):
        return remote(
            sib_got.at[0, which, piece], ring.at[which, piece],
            far_ssem.at[which, piece], far_rsem.at[which, piece], col=(up, down)[piece % 2],
        )

    def near_copy(which, way, piece):
        return remote(
            sib_got.at[1 + way, which, piece], (from_left, from_right)[way].at[which, piece],
            near_ssem.at[which, way, piece], near_rsem.at[which, way, piece], col=(up, down)[way],
        )

    def z_copy(piece):
        return remote(z_sent.at[piece], z_got.at[piece], z_ssem.at[piece], z_rsem.at[piece], col=z_peer)

    def join(place, which):
        target = (x_far, x_up, x_down, x)[place]
        half_z = 1 - zh if which == 0 else zh
        sib_copy(place, which).wait_recv()
        sib_got[place, which] += part_ref[target * 4 + half_z * 2 + core]

    def open_ring(which):
        join(0, which)
        for piece in range(LAYER_PIECES):
            far_copy(which, piece).start()
        for way in (0, 1):
            join(1 + way, which)
            near_copy(which, way, 1 - way).start()
        join(3, which)

    def relay_ring(which, pieces):
        for piece in pieces:
            way = piece % 2
            far_copy(which, piece).wait_recv()
            sib_got[1 + way, which, piece] += ring[which, piece]
            near_copy(which, way, piece).start()

    def rest_ring(which):
        for way, piece in after:
            near_copy(which, way, piece).start()

    def ring_total(which, piece):
        for way in (0, 1):
            near_copy(which, way, piece).wait_recv()
        return sib_got[3, which, piece] + from_left[which, piece] + from_right[which, piece]

    def send_over(pieces):
        for piece in pieces:
            z_sent[piece] = ring_total(0, piece)
            z_copy(piece).start()

    wait_for_all()
    for which in (0, 1):
        for place in range(4):
            target = (x_far, x_up, x_down, x)[place] * 4 + (1 - zh if which == 0 else zh) * 2
            take_block(info_ref, sums, part_ref, target + 1 - core)
            sib_copy(place, which).start()
            take_block(info_ref, sums, part_ref, target + core)
    open_ring(0)
    relay_ring(0, first)
    rest_ring(0)
    relay_ring(0, rest)
    open_ring(1)
    send_over(first)
    relay_ring(1, first)
    rest_ring(1)
    send_over(rest)
    relay_ring(1, rest)

    def spread_z(piece):
        return remote(
            held.at[col, piece], held.at[col, piece], zg_sem.at[piece], recv_sem.at[col, piece], col=z_peer
        )

    def spread_x(which, way, piece):
        half_z = zh if which == 0 else 1 - zh
        block = x * 4 + half_z * 2 + core
        return remote(
            held.at[block, piece], held.at[block, piece], xg_sem.at[which, way, piece], recv_sem.at[block, piece],
            col=(up, down)[way],
        )

    def relay_x(which, piece):
        half_z = zh if which == 0 else 1 - zh
        way = piece % 2
        block = (x_down, x_up)[way] * 4 + half_z * 2 + core
        return remote(
            held.at[block, piece], held.at[block, piece], relay_sem.at[which, piece], recv_sem.at[block, piece],
            col=(up, down)[way],
        )

    def spread_sib(place, which, piece):
        target = (x, x_up, x_down, x_far)[place]
        half_z = zh if which == 0 else 1 - zh
        block = target * 4 + half_z * 2 + core
        return remote(
            held.at[block, piece], held.at[block, piece], sg_sem.at[place, which, piece], recv_sem.at[block, piece],
            col=sibling,
        )

    def arrived(block, piece):
        remote(
            held.at[block, piece], held.at[block, piece], zg_sem.at[piece], recv_sem.at[block, piece], col=sibling
        ).wait_recv()

    def spread(which, piece):
        way = piece % 2
        spread_x(which, way, piece).start()
        spread_x(which, 1 - way, piece).start()
        spread_sib(0, which, piece).start()

    def settle(block, piece):
        put_pair(pair_ref, block, piece, LAYER_PIECES, held[block, piece])

    for piece, scale in enumerate(piece_columns(scale_ref, 2 * col, LAYER_PIECES)):
        here = slice(piece * part_ref.shape[2], (piece + 1) * part_ref.shape[2])
        own = ring_total(1, piece)
        z_copy(piece).wait_recv()
        aggregated = (own + z_got[piece]) * scale
        preact = jnp.dot(split_columns(aggregated), w_fore[...], preferred_element_type=F32) + b_ref[...]
        logistic = 1.0 / (1.0 + jnp.exp(-preact))
        pre_grad = grad_ref[here, :] * logistic * (1.0 + preact * (1.0 - logistic))
        held[col, piece] = scale * jnp.dot(split_columns(pre_grad), w_back[...], preferred_element_type=F32)
        spread_z(piece).start()
        spread(0, piece)
        act_ref[here, :] = preact * logistic
        aggs[here, :] = aggregated
        grads[here, :] = pre_grad

    weight_part = lax.dot_general(
        split_rows(aggs[...], (0, 1, 0)), split_rows(grads[...], (0, 0, 1)), TN, preferred_element_type=F32
    )
    bias_part = jnp.broadcast_to(jnp.sum(grads[...], axis=0, keepdims=True), (8, TILE))
    for part in range(16):
        wgrad[part, 0:8, :] = weight_part[part * 8 : part * 8 + 8]
        wgrad[part, 8:16, :] = bias_part

    def w_copy(distance):
        peer = lax.rem(col + distance, 16)
        return remote(
            wgrad.at[peer], w_got.at[distance - 1], w_ssem.at[distance - 1], w_rsem.at[distance - 1], col=peer
        )

    for distance in range(1, 16):
        w_copy(distance).start()

    def relay(which, pieces):
        half_z = zh if which == 0 else 1 - zh
        for piece in pieces:
            way = piece % 2
            arrived((x_down, x_up)[way] * 4 + half_z * 2 + core, piece)
            relay_x(which, piece).start()
            spread_sib((2, 1)[way], which, piece).start()

    def near_rest(which):
        half_z = zh if which == 0 else 1 - zh
        for piece in range(LAYER_PIECES):
            way = piece % 2
            arrived((x_up, x_down)[way] * 4 + half_z * 2 + core, piece)
            spread_sib((1, 2)[way], which, piece).start()

    def far_rest(which):
        half_z = zh if which == 0 else 1 - zh
        for piece in range(LAYER_PIECES):
            arrived(x_far * 4 + half_z * 2 + core, piece)
            spread_sib(3, which, piece).start()

    other = x * 4 + (1 - zh) * 2 + core

    def take_over(piece):
        arrived(other, piece)
        spread(1, piece)

    relay(0, range(LAYER_PIECES))
    near_rest(0)
    for piece in range(LAYER_PIECES):
        take_over(piece)
        if piece == 1:
            far_rest(0)
        if piece >= 2:
            relay(1, (piece - 2,))
    for piece in range(max(LAYER_PIECES - 2, 0), LAYER_PIECES - 1):
        relay(1, (piece,))
    for side in (x, x_up):
        for piece in range(LAYER_PIECES):
            settle(side * 4 + zh * 2 + core, piece)
    relay(1, (LAYER_PIECES - 1,))
    for side in (x_down, x_far):
        for piece in range(LAYER_PIECES):
            settle(side * 4 + zh * 2 + core, piece)
    near_rest(1)
    for side in (x, x_up, x_down, x_far):
        for piece in range(LAYER_PIECES):
            block = side * 4 + zh * 2 + 1 - core
            arrived(block, piece)
            settle(block, piece)
    far_rest(1)
    for side in (x, x_up, x_down, x_far):
        for piece in range(LAYER_PIECES):
            settle(side * 4 + (1 - zh) * 2 + core, piece)
            block = side * 4 + (1 - zh) * 2 + 1 - core
            arrived(block, piece)
            settle(block, piece)

    wsum = wgrad[col]
    for distance in range(1, 16):
        w_copy(distance).wait_recv()
        wsum += w_got[distance - 1]
    wsum_ref[...] = wsum
    for which in (0, 1):
        for place in range(4):
            sib_copy(place, which).wait_send()
            for piece in range(LAYER_PIECES):
                spread_sib(place, which, piece).wait_send()
        for piece in range(LAYER_PIECES):
            far_copy(which, piece).wait_send()
            relay_x(which, piece).wait_send()
            for way in (0, 1):
                near_copy(which, way, piece).wait_send()
                spread_x(which, way, piece).wait_send()
    for piece in range(LAYER_PIECES):
        z_copy(piece).wait_send()
        spread_z(piece).wait_send()
    for distance in range(1, 16):
        w_copy(distance).wait_send()


def dense_layer(count, info, tiles, pairs, weight, bias_vector, out_grad, dst_scale):
    dma = pltpu.SemaphoreType.DMA
    block = block_of(LAYER_PIECES)
    return pl.pallas_call(
        layer_kernel,
        in_specs=[pl.BlockSpec(memory_space=pltpu.SMEM)] * 2 + [VMEM_SPEC] * 6,
        out_specs=[VMEM_SPEC] * 3,
        out_shape=[
            jax.ShapeDtypeStruct((2 * TILE, TILE), F32),
            jax.ShapeDtypeStruct((32, TILE, 2 * TILE), BF16),
            jax.ShapeDtypeStruct(SLICE, F32),
        ],
        scratch_shapes=[
            pltpu.VMEM(tiles.shape, F32),
            pltpu.VMEM((16,) + block, F32),
            pltpu.VMEM((3 * TILE, TILE), BF16),
            pltpu.VMEM((3 * TILE, TILE), BF16),
            pltpu.VMEM((4, 2) + block, F32),
            pltpu.VMEM((2,) + block, F32),
            pltpu.VMEM((2,) + block, F32),
            pltpu.VMEM((2,) + block, F32),
            pltpu.VMEM(block, F32),
            pltpu.VMEM(block, F32),
            pltpu.VMEM((16,) + block, F32),
            pltpu.VMEM((2 * TILE, TILE), F32),
            pltpu.VMEM((2 * TILE, TILE), F32),
            pltpu.VMEM((16,) + SLICE, F32),
            pltpu.VMEM((15,) + SLICE, F32),
            dma((4, 2)), dma((4, 2)), dma((2, LAYER_PIECES)), dma((2, LAYER_PIECES)),
            dma((2, 2, LAYER_PIECES)), dma((2, 2, LAYER_PIECES)), dma((LAYER_PIECES,)), dma((LAYER_PIECES,)),
            dma((16, LAYER_PIECES)), dma((LAYER_PIECES,)), dma((2, 2, LAYER_PIECES)), dma((2, LAYER_PIECES)), dma((4, 2, LAYER_PIECES)),
            dma((15,)), dma((15,)),
        ],
        compiler_params=pltpu.CompilerParams(vmem_limit_bytes=LIMIT, collective_id=1, has_side_effects=True),
        name="dense_layer",
    )(count, info, tiles, pairs, weight, bias_vector.reshape(1, TILE), out_grad, dst_scale)


def scatter_kernel(
    count_ref, info_ref, tiles_ref, source_ref, wsum_ref, scale_ref, grad_ref, wgrad_ref, bgrad_ref,
    sums, part_ref, staged, ring, from_down, from_up, total, line_up, line_down, w_got, w_all,
    far_ssem, far_rsem, near_ssem, near_rsem, line_ssem, line_rsem, w_ssem, w_rsem, all_ssem, all_rsem,
):
    row, col = lax.axis_index("row"), lax.axis_index("col")
    y, z = lax.div(row, 4), lax.rem(row, 4)
    y_up, y_down, y_far = lax.rem(y + 1, 4), lax.rem(y + 3, 4), lax.rem(y + 2, 4)
    wait_for_all = greet(
        [lax.rem(row + d, 16) for d in range(1, 16)], [lax.rem(col + d, 16) for d in range(1, 16)]
    )
    up, down = y_up * 4 + z, y_down * 4 + z

    def far_copy(zb, piece):
        return remote(
            part_ref.at[y_far * 4 + zb, piece], ring.at[zb, piece],
            far_ssem.at[zb, piece], far_rsem.at[zb, piece], row=(up, down)[piece % 2],
        )

    def near_copy(zb, way, piece):
        block = (y_up, y_down)[way] * 4 + zb
        source = staged.at[zb, piece] if piece % 2 == way else part_ref.at[block, piece]
        return remote(
            source, (from_down, from_up)[way].at[zb, piece],
            near_ssem.at[zb, way, piece], near_rsem.at[zb, way, piece], row=(up, down)[way],
        )

    def line_copy(zb, way, piece):
        return remote(
            total.at[zb, piece], (line_up, line_down)[way].at[zb, piece],
            line_ssem.at[zb, piece], line_rsem.at[zb, way, piece],
            row=y * 4 + lax.rem(z + (1 if way == 0 else 3), 4),
        )

    def w_copy(distance):
        return remote(
            wsum_ref, w_got.at[row], w_ssem.at[distance - 1], w_rsem.at[row], row=lax.rem(row + distance, 16)
        )

    def w_arrived(distance):
        sender = lax.rem(row + distance, 16)
        remote(wsum_ref, w_got.at[sender], w_ssem.at[distance - 1], w_rsem.at[sender], row=sender).wait_recv()

    def all_copy(distance):
        return remote(
            w_all.at[col], w_all.at[col], all_ssem.at[distance - 1], all_rsem.at[col], col=lax.rem(col + distance, 16)
        )

    def all_arrived(distance):
        sender = lax.rem(col + distance, 16)
        remote(
            w_all.at[sender], w_all.at[sender], all_ssem.at[distance - 1], all_rsem.at[sender], col=sender
        ).wait_recv()

    def w_total():
        for distance in range(1, 16):
            w_arrived(distance)
        whole = w_got[0]
        for sender in range(1, 16):
            whole += w_got[sender]
        w_all[col] = whole
        for distance in range(1, 16):
            all_copy(distance).start()

    zbs = [in_order(INWARD, place, z) for place in range(4)]

    def far_step(place):
        for piece in range(SCATTER_PIECES):
            far_copy(zbs[place], piece).start()

    def near_step(place, pieces):
        for way in (0, 1):
            for piece in pieces:
                if piece % 2 != way:
                    near_copy(zbs[place], way, piece).start()

    def relay_step(place, pieces):
        zb = zbs[place]
        for piece in pieces:
            way = piece % 2
            far_copy(zb, piece).wait_recv()
            staged[zb, piece] = part_ref[(y_up, y_down)[way] * 4 + zb, piece] + ring[zb, piece]
            near_copy(zb, way, piece).start()

    def line_ways(place):
        zb = zbs[place]
        if place == 3:
            return ((0, z > 0, None), (1, z < 3, None))
        return ((0, (zb > z) & (z > 0), zb > z), (1, (zb < z) & (z < 3), zb < z))

    def close_step(place):
        zb = zbs[place]
        for piece in range(SCATTER_PIECES):
            for way in (0, 1):
                near_copy(zb, way, piece).wait_recv()
            total[zb, piece] = part_ref[y * 4 + zb, piece] + from_down[zb, piece] + from_up[zb, piece]
            for way, comes, goes in line_ways(place):

                @pl.when(comes)
                def _():
                    line_copy(zb, way, piece).wait_recv()
                    total[zb, piece] += (line_up, line_down)[way][zb, piece]

                if goes is not None:
                    pl.when(goes)(lambda: line_copy(zb, way, piece).start())

    def send_step(place):
        zb = zbs[place]
        for piece in range(SCATTER_PIECES):
            far_copy(zb, piece).wait_send()
            for way in (0, 1):
                near_copy(zb, way, piece).wait_send()
        for way, _, goes in line_ways(place):
            for piece in range(SCATTER_PIECES):
                if goes is not None:
                    pl.when(goes)(lambda: line_copy(zb, way, piece).wait_send())

    def product_part(first, last, so_far):
        return block_product(TN, count_ref, info_ref, tiles_ref, source_ref, sums, first, last, so_far)

    groups = tiles_ref.shape[0] // 8
    so_far = product_part(0, groups // 2, jnp.zeros((TILE, TILE), F32))
    wait_for_all()
    for distance in range(1, 16):
        w_copy(distance).start()
    w_got[row] = wsum_ref[...]
    product_part(groups // 2, groups, so_far)
    for place in range(4):
        take_block(info_ref, sums, part_ref, y_far * 4 + zbs[place])
        if place == 0:
            far_step(0)
        for side in (y_up, y_down):
            take_block(info_ref, sums, part_ref, side * 4 + zbs[place])
        if place == 0:
            near_step(0, range(SCATTER_PIECES))
        if place == 1:
            far_step(1)
        take_block(info_ref, sums, part_ref, y * 4 + zbs[place])
    for place in range(4):
        relay_step(place, range(SCATTER_PIECES))
        if place < 3:
            near_step(place + 1, range(SCATTER_PIECES))
        if place < 2:
            far_step(place + 2)
        if place:
            close_step(place - 1)
        if place == 1:
            w_total()
    close_step(3)

    for piece, scale in enumerate(piece_columns(scale_ref, 2 * row, SCATTER_PIECES)):
        grad_ref[pl.ds(piece * scale.shape[0], scale.shape[0]), :] = total[z, piece] * scale
    for distance in range(1, 16):
        all_arrived(distance)
    for part in range(16):
        wgrad_ref[part * 8 : part * 8 + 8, :] = w_all[part, 0:8, :]
    bgrad_ref[...] = w_all[0, 8:9, :]
    for place in range(4):
        send_step(place)
    for distance in range(1, 16):
        w_copy(distance).wait_send()
        all_copy(distance).wait_send()


def scatter_gradients(count, info, tiles, pairs, wsum, src_scale):
    dma = pltpu.SemaphoreType.DMA
    block = block_of(SCATTER_PIECES)
    return pl.pallas_call(
        scatter_kernel,
        in_specs=[pl.BlockSpec(memory_space=pltpu.SMEM)] * 2 + [VMEM_SPEC] * 4,
        out_specs=[VMEM_SPEC] * 3,
        out_shape=[
            jax.ShapeDtypeStruct((2 * TILE, TILE), F32),
            jax.ShapeDtypeStruct((TILE, TILE), F32),
            jax.ShapeDtypeStruct((1, TILE), F32),
        ],
        scratch_shapes=[pltpu.VMEM(tiles.shape, F32), pltpu.VMEM((16,) + block, F32)]
        + [pltpu.VMEM((4,) + block, F32)] * 7
        + [
            pltpu.VMEM((16,) + SLICE, F32),
            pltpu.VMEM((16,) + SLICE, F32),
            dma((4, SCATTER_PIECES)), dma((4, SCATTER_PIECES)), dma((4, 2, SCATTER_PIECES)), dma((4, 2, SCATTER_PIECES)),
            dma((4, SCATTER_PIECES)), dma((4, 2, SCATTER_PIECES)), dma((15,)), dma((16,)), dma((15,)), dma((16,)),
        ],
        compiler_params=pltpu.CompilerParams(vmem_limit_bytes=LIMIT, collective_id=2, has_side_effects=True),
        name="scatter_gradients",
    )(count, info, tiles, pairs, wsum, src_scale)


def put_kernel(*refs):
    count = len(refs) // 2
    ins, outs, sems = refs[:count], refs[count : 2 * count], refs[-1]
    copies = [pltpu.make_async_copy(ins[k], outs[k], sems.at[k]) for k in range(count)]
    for copy in copies:
        copy.start()
    for copy in copies:
        copy.wait()


def put_out(*arrays):
    return pl.pallas_call(
        put_kernel,
        in_specs=[VMEM_SPEC] * len(arrays),
        out_specs=[pl.BlockSpec(memory_space=pltpu.HBM)] * len(arrays),
        out_shape=[jax.ShapeDtypeStruct(array.shape, array.dtype) for array in arrays],
        scratch_shapes=[pltpu.SemaphoreType.DMA((len(arrays),))],
        compiler_params=pltpu.CompilerParams(vmem_limit_bytes=LIMIT),
        name="put_out",
    )(*arrays)


def local(features, weight, bias_vector, out_grad, adj_tiles, tile_slots, tile_counts):
    tiles, pairs, src_scale, dst_scale, forward_info, backward_info = gather_features(
        features, adj_tiles[0, 0], tile_slots[0], tile_counts
    )
    activated, grad_pairs, wsum = dense_layer(
        tile_counts, forward_info, tiles, pairs, weight, bias_vector, out_grad, dst_scale
    )
    feature_grad, weight_grad, bias_grad = scatter_gradients(
        tile_counts, backward_info, tiles, grad_pairs, wsum, src_scale
    )
    activated, feature_grad, weight_grad, bias_grad = put_out(activated, feature_grad, weight_grad, bias_grad)
    return activated, feature_grad, weight_grad, bias_grad.reshape(TILE)


def solution(mesh):
    return jax.shard_map(
        local,
        mesh=mesh,
        in_specs=(
            P(("col", "row"), None),
            P(),
            P(),
            P(("row", "col"), None),
            P("row", "col", None, None, None),
            P("row", "col", None),
            P("row", "col"),
        ),
        out_specs=(P(("row", "col"), None), P(("col", "row"), None), P(), P()),
        check_vma=False,
    )
```

time: 117 us -> 114 us (0.974); the launches traced: 118 us -> 112 us
  local copies, waits for them, and re-layouts: 3.12 us -> 0.01 us
  Pallas kernels: 113 us -> 111 us
    pallas_call x4 -> x3, Pallas kernels: 81.9 us -> 76.3 us  [the longest x1 46.4 us: dense_layer(): pl.pallas_call(layer_kernel, in_specs=[pl.BlockSpec(memory_space=pltpu.SM...]
    pallas_call x1, Pallas kernels: 31.1 us -> 34.5 us  [gather_features(): pl.pallas_call(gather_kernel, in_specs=[pl.BlockSpec(memory_space=pltpu.S...]
    unnamed x12 -> x6, local copies, waits for them, and re-layouts: 3.12 us -> 0.01 us
where the time goes in v3:
time: 114 us; the launch traced here: 112 us
  Pallas kernels  111 us (97%)
  between operations  1.35 us (1%)
    pallas_call x1, Pallas kernels, dense_layer(): pl.pallas_call(layer_kernel, in_specs=[pl.BlockSpec(memory_space=pltpu.SM...  46.4 us
    pallas_call x1, Pallas kernels, gather_features(): pl.pallas_call(gather_kernel, in_specs=[pl.BlockSpec(memory_space=pltpu.S...  34.5 us
    pallas_call x1, Pallas kernels, scatter_gradients(): pl.pallas_call(scatter_kernel, in_specs=[pl.BlockSpec(memory_space=pltpu....  29.2 us

profile of v3, /device:TPU:1, one launch (start us, length us, event | category | flops | bytes accessed | tf_op | source)
XLA Modules:
  0.0 112.1 jit_solution(13684404574345774896)
XLA Ops:
  1.3 0.0 copy-start
  1.3 0.0 copy-start.1
  1.3 0.0 copy-start.2
  1.3 34.5 %gather_features.1 = (bf16[128,128,128]{2,1,0:T(8,128)(2,1)S(1)}, bf16[32,128,256]{2,1,0:T(8,128)(2,1)S(1)}, f32[32,128]{1,0:T(8,128)S(1)}, f32[32,128]{1,0:T(8,...) custom-call(s32[1,1]{1,0:T(1,128)S(6)} %copy.11.count_ref, s32[1,128]{1,0:T(1,128)} %bitcast.8, ...), custom_call_target="tpu_custom_call" | custom-call | tf_op jit(solution)/shard_map/gather_features/pallas_call | solution.py:356
  35.8 0.0 copy-done
  35.8 0.0 copy-done.1
  35.8 0.0 copy-done.2
  35.8 46.4 %dense_layer.1 = (f32[256,128]{1,0:T(8,128)S(1)}, bf16[32,128,256]{2,1,0:T(8,128)(2,1)S(1)}, f32[16,128]{1,0:T(8,128)S(1)}) custom-call(s32[1,1]{1,0:T(1,128)S(6)} %copy.11.count_ref, s32[5,128]{1,0:T(8,128)S(1)} %get-tuple-element.20.info_ref, bf16[128,128,128]{2,1,0:T(8,128)(2,1)S(1)} %get-tuple-element.21.tiles_ref, ...), custom_call_target="tpu_custom_call" | custom-call | tf_op jit(solution)/shard_map/dense_layer/pallas_call | solution.py:663
  82.2 29.2 %scatter_gradients.1 = (f32[256,128]{1,0:T(8,128)S(1)}, f32[128,128]{1,0:T(8,128)S(1)}, f32[1,128]{1,0:T(1,128)S(1)}) custom-call(s32[1,1]{1,0:T(1,128)S(6)} %copy.11.count_ref, s32[5,128]{1,0:T(8,128)S(1)} %get-tuple-element.25.info_ref, bf16[128,128,128]{2,1,0:T(8,128)(2,1)S(1)} %get-tuple-element.21.tiles_ref, ...), custom_call_target="tpu_custom_call" | custom-call | tf_op jit(solution)/shard_map/scatter_gradients/pallas_call | solution.py:865
  111.4 0.8 put_out.1
Async XLA Ops:
  1.3 34.5 %copy-start = (f32[256,128]{1,0:T(8,128)S(1)}, f32[256,128]{1,0:T(8,128)}, u32[]{:S(2)}) copy-start(f32[256,128]{1,0:T(8,128)} %grad_ref.1) | copy-start | bytes 393220
  1.3 34.5 %copy-start.1 = (f32[128,128]{1,0:T(8,128)S(1)}, f32[128,128]{1,0:T(8,128)}, u32[]{:S(2)}) copy-start(f32[128,128]{1,0:T(8,128)} %w_ref.1) | copy-start | bytes 196612
  1.3 34.5 %copy-start.2 = (f32[128]{0:T(128)S(1)}, f32[128]{0:T(128)}, u32[]{:S(2)}) copy-start(f32[128]{0:T(128)} %param.9) | copy-start | bytes 1540

commit v4 on v3

--- a/solution.py
+++ b/solution.py
@@ -293,14 +293,13 @@
             if step < 3:
                 degree_copy(which, step + 1).start()
 
-    degree_chunks(0, chunks // 4)
     feat_copy.wait()
     wait_for_all()
     column_step(0)
-    degree_chunks(chunks // 4, chunks // 2 + 2)
+    degree_chunks(0, chunks // 2)
     relay_step(0)
     column_step(1)
-    degree_chunks(chunks // 2 + 2, chunks)
+    degree_chunks(chunks // 2, chunks)
     degree_parts()
     for which in (0, 1):
         degree_copy(which, 0).start()
@@ -841,7 +840,7 @@
             far_step(place + 2)
         if place:
             close_step(place - 1)
-        if place == 1:
+        if place == 2:
             w_total()
     close_step(3)
 

time: 114 us -> 115 us (level)
  Pallas kernels: 111 us -> 113 us
    pallas_call x1, Pallas kernels: 29.2 us -> 31.1 us  [scatter_gradients(): pl.pallas_call(scatter_kernel, in_specs=[pl.BlockSpec(memory_space=pltpu....]
where the time goes in v4:
time: 115 us; the launch traced here: 114 us
  Pallas kernels  113 us (98%)
  between operations  1.35 us (1%)
    pallas_call x1, Pallas kernels, dense_layer(): pl.pallas_call(layer_kernel, in_specs=[pl.BlockSpec(memory_space=pltpu.SM...  47.2 us
    pallas_call x1, Pallas kernels, gather_features(): pl.pallas_call(gather_kernel, in_specs=[pl.BlockSpec(memory_space=pltpu.S...  33.6 us
    pallas_call x1, Pallas kernels, scatter_gradients(): pl.pallas_call(scatter_kernel, in_specs=[pl.BlockSpec(memory_space=pltpu....  31.1 us

profile of v4, /device:TPU:1, one launch (start us, length us, event | category | flops | bytes accessed | tf_op | source)
XLA Modules:
  0.0 114.0 jit_solution(5542311458512130887)
XLA Ops:
  1.3 0.0 copy-start
  1.3 0.0 copy-start.1
  1.3 0.0 copy-start.2
  1.3 33.6 %gather_features.1 = (bf16[128,128,128]{2,1,0:T(8,128)(2,1)S(1)}, bf16[32,128,256]{2,1,0:T(8,128)(2,1)S(1)}, f32[32,128]{1,0:T(8,128)S(1)}, f32[32,128]{1,0:T(8,...) custom-call(s32[1,1]{1,0:T(1,128)S(6)} %copy.11.count_ref, s32[1,128]{1,0:T(1,128)} %bitcast.8, ...), custom_call_target="tpu_custom_call" | custom-call | tf_op jit(solution)/shard_map/gather_features/pallas_call | solution.py:355
  34.9 0.0 copy-done
  34.9 0.0 copy-done.1
  34.9 0.0 copy-done.2
  35.0 47.2 %dense_layer.1 = (f32[256,128]{1,0:T(8,128)S(1)}, bf16[32,128,256]{2,1,0:T(8,128)(2,1)S(1)}, f32[16,128]{1,0:T(8,128)S(1)}) custom-call(s32[1,1]{1,0:T(1,128)S(6)} %copy.11.count_ref, s32[5,128]{1,0:T(8,128)S(1)} %get-tuple-element.20.info_ref, bf16[128,128,128]{2,1,0:T(8,128)(2,1)S(1)} %get-tuple-element.21.tiles_ref, ...), custom_call_target="tpu_custom_call" | custom-call | tf_op jit(solution)/shard_map/dense_layer/pallas_call | solution.py:662
  82.1 31.1 %scatter_gradients.1 = (f32[256,128]{1,0:T(8,128)S(1)}, f32[128,128]{1,0:T(8,128)S(1)}, f32[1,128]{1,0:T(1,128)S(1)}) custom-call(s32[1,1]{1,0:T(1,128)S(6)} %copy.11.count_ref, s32[5,128]{1,0:T(8,128)S(1)} %get-tuple-element.25.info_ref, bf16[128,128,128]{2,1,0:T(8,128)(2,1)S(1)} %get-tuple-element.21.tiles_ref, ...), custom_call_target="tpu_custom_call" | custom-call | tf_op jit(solution)/shard_map/scatter_gradients/pallas_call | solution.py:864
  113.2 0.8 put_out.1
Async XLA Ops:
  1.3 33.7 %copy-start = (f32[256,128]{1,0:T(8,128)S(1)}, f32[256,128]{1,0:T(8,128)}, u32[]{:S(2)}) copy-start(f32[256,128]{1,0:T(8,128)} %grad_ref.1) | copy-start | bytes 393220
  1.3 33.7 %copy-start.1 = (f32[128,128]{1,0:T(8,128)S(1)}, f32[128,128]{1,0:T(8,128)}, u32[]{:S(2)}) copy-start(f32[128,128]{1,0:T(8,128)} %w_ref.1) | copy-start | bytes 196612
  1.3 33.7 %copy-start.2 = (f32[128]{0:T(128)S(1)}, f32[128]{0:T(128)}, u32[]{:S(2)}) copy-start(f32[128]{0:T(128)} %param.9) | copy-start | bytes 1540

commit v5 on v4

--- a/solution.py
+++ b/solution.py
@@ -16,6 +16,7 @@
 CHUNK = 8
 LIMIT = 24 << 20
 GATHER_PIECES = 2
+GATHER_ROWS = ((0, 96), (96, 96), (192, 64))
 LAYER_PIECES = 2
 SCATTER_PIECES = 2
 
@@ -163,7 +164,7 @@
     count_ref, slots_ref, feat_ref, adj_ref,
     tiles_ref, pair_ref, src_scale_ref, dst_scale_ref, forward_info_ref, backward_info_ref,
     adj_got, row_sums, col_sums, parts, held, slots_got, deg_sent, deg_got,
-    feat_sem, adj_sem, recv_sem, z_sem, y_sem, relay_sem, deg_send_sem, deg_recv_sem,
+    feat_sem, adj_sem, recv_sem, z_sem, y_sem, relay_sem, across_sem, along_sem, deg_send_sem, deg_recv_sem,
 ):
     chunks = adj_ref.shape[0] // CHUNK
     row, col = lax.axis_index("row"), lax.axis_index("col")
@@ -218,10 +219,13 @@
         parts[0] = jnp.dot(col_select, col_sums[...].astype(BF16), preferred_element_type=F32)
         parts[1] = jnp.dot(row_select, row_sums[...].astype(BF16), preferred_element_type=F32)
 
+    def part_of(block, piece):
+        return held.at[block, pl.ds(*GATHER_ROWS[piece])]
+
     def z_copy(z_from, way, piece):
         block = y * 4 + z_from
         return remote(
-            held.at[block, piece], held.at[block, piece],
+            part_of(block, piece), part_of(block, piece),
             z_sem.at[z_from, way, piece], recv_sem.at[block, piece],
             row=y * 4 + lax.rem(z + (1 if way == 0 else 3), 4),
         )
@@ -229,7 +233,7 @@
     def y_copy(z_from, way, piece):
         block = y * 4 + z_from
         return remote(
-            held.at[block, piece], held.at[block, piece],
+            part_of(block, piece), part_of(block, piece),
             y_sem.at[z_from, way, piece], recv_sem.at[block, piece],
             row=(y_up, y_down)[way] * 4 + z,
         )
@@ -238,14 +242,14 @@
         way = piece % 2
         block = (y_down, y_up)[way] * 4 + z_from
         return remote(
-            held.at[block, piece], held.at[block, piece],
+            part_of(block, piece), part_of(block, piece),
             relay_sem.at[z_from, piece], recv_sem.at[block, piece],
             row=(y_up, y_down)[way] * 4 + z,
         )
 
     def arrived(block, piece):
         remote(
-            held.at[block, piece], held.at[block, piece], relay_sem.at[0, piece], recv_sem.at[block, piece],
+            part_of(block, piece), part_of(block, piece), relay_sem.at[0, piece], recv_sem.at[block, piece],
             row=y_up * 4 + z,
         ).wait_recv()
 
@@ -270,6 +274,36 @@
         for way, piece in by_way(GATHER_PIECES):
             y_copy(z_from, way, piece).start()
 
+    def across_copy(place):
+        return remote(
+            part_of(row, 2), part_of(row, 2), across_sem.at[place], recv_sem.at[row, 2],
+            row=(y_up, y_down, y_far)[place] * 4 + z,
+        )
+
+    def along_copy(turn, z_from, way):
+        block = lax.rem(y + turn, 4) * 4 + z_from
+        return remote(
+            part_of(block, 2), part_of(block, 2), along_sem.at[turn, z_from, way], recv_sem.at[block, 2],
+            row=y * 4 + lax.rem(z + (1 if way == 0 else 3), 4),
+        )
+
+    def along_step(place, turns, action, wait=True):
+        z_from = in_order(OUTWARD, place, z)
+        for turn in turns:
+            if wait and (place or turn):
+                arrived(lax.rem(y + turn, 4) * 4 + z_from, 2)
+            for way in (0, 1):
+                goes = z < 3 if way == 0 else z > 0
+                if place:
+                    goes = goes & (z_from < z if way == 0 else z_from > z)
+                pl.when(goes)(lambda: action(along_copy(turn, z_from, way)))
+
+    def start(copy):
+        copy.start()
+
+    def wait_send(copy):
+        copy.wait_send()
+
     def relay_step(place):
         z_from = in_order(OUTWARD, place, z)
         for piece in range(GATHER_PIECES):
@@ -295,17 +329,23 @@
 
     feat_copy.wait()
     wait_for_all()
+    for place in range(3):
+        across_copy(place).start()
     column_step(0)
+    along_step(0, (0,), start)
     degree_chunks(0, chunks // 2)
+    along_step(0, (1, 3, 2), start)
     relay_step(0)
     column_step(1)
     degree_chunks(chunks // 2, chunks)
     degree_parts()
     for which in (0, 1):
         degree_copy(which, 0).start()
+    along_step(1, range(4), start)
     relay_step(1)
     column_step(2)
     degree_step(0)
+    along_step(2, range(4), start)
     relay_step(2)
     degree_step(1)
     column_step(3)
@@ -314,14 +354,15 @@
         for place, line in enumerate(sort_table(slots, live, by_row)):
             info_ref[place : place + 1, :] = line
     relay_step(3)
+    along_step(3, range(4), start)
     degree_step(3)
 
     src_scale_ref[...] = lax.rsqrt(1.0 + deg_sent[0, 3])
     dst_scale_ref[...] = lax.rsqrt(1.0 + deg_sent[1, 3])
 
     def settle(block):
-        for piece, scale in enumerate(piece_columns(src_scale_ref, 2 * block, GATHER_PIECES)):
-            put_pair(pair_ref, block, piece, GATHER_PIECES, held[block, piece] * scale)
+        for half, scale in enumerate(piece_columns(src_scale_ref, 2 * block, 2)):
+            put_pair(pair_ref, block, half, 2, held[block, half * TILE : half * TILE + TILE, :] * scale)
 
     for place in range(4):
         settle(y * 4 + in_order(OUTWARD, place, z))
@@ -344,6 +385,9 @@
                 y_copy(z_from, way, piece).wait_send()
             relay_copy(z_from, piece).wait_send()
         on_line(place, range(GATHER_PIECES), lambda copy: copy.wait_send())
+        along_step(place, range(4), wait_send, wait=False)
+    for place in range(3):
+        across_copy(place).wait_send()
     for which in (0, 1):
         for step in range(4):
             degree_copy(which, step).wait_send()
@@ -374,16 +418,18 @@
             pltpu.VMEM((slot_total, TILE), F32),
             pltpu.VMEM((slot_total, TILE), F32),
             pltpu.VMEM((2, 32, TILE), F32),
-            pltpu.VMEM((16,) + block_of(GATHER_PIECES), F32),
+            pltpu.VMEM((16, 2 * TILE, TILE), F32),
             pltpu.VMEM((1, TILE), jnp.int32),
             pltpu.VMEM((2, 4, 32, TILE), F32),
             pltpu.VMEM((2, 4, 32, TILE), F32),
             dma((2,)),
             dma((slot_total // CHUNK,)),
-            dma((16, GATHER_PIECES)),
+            dma((16, 3)),
             dma((4, 2, GATHER_PIECES)),
             dma((4, 2, GATHER_PIECES)),
             dma((4, GATHER_PIECES)),
+            dma((3,)),
+            dma((4, 4, 2)),
             dma((2, 4)),
             dma((2, 4)),
         ],
@@ -392,7 +438,7 @@
     )(
         count,
         pltpu.with_memory_space_constraint(slots, pltpu.HBM),
-        pltpu.with_memory_space_constraint(features.reshape(block_of(GATHER_PIECES)), pltpu.HBM),
+        pltpu.with_memory_space_constraint(features, pltpu.HBM),
         pltpu.with_memory_space_constraint(adj_tiles, pltpu.HBM),
     )
 
@@ -840,7 +886,7 @@
             far_step(place + 2)
         if place:
             close_step(place - 1)
-        if place == 2:
+        if place == 0:
             w_total()
     close_step(3)
 

time: 115 us -> 113 us (0.983)
  Pallas kernels: 113 us -> 111 us
    pallas_call x1, Pallas kernels: 31.1 us -> 28.5 us  [scatter_gradients(): pl.pallas_call(scatter_kernel, in_specs=[pl.BlockSpec(memory_space=pltpu....]
where the time goes in v5:
time: 113 us; the launch traced here: 112 us
  Pallas kernels  111 us (98%)
  between operations  1.35 us (1%)
    pallas_call x1, Pallas kernels, dense_layer(): pl.pallas_call(layer_kernel, in_specs=[pl.BlockSpec(memory_space=pltpu.SM...  48.1 us
    pallas_call x1, Pallas kernels, gather_features(): pl.pallas_call(gather_kernel, in_specs=[pl.BlockSpec(memory_space=pltpu.S...  33.4 us
    pallas_call x1, Pallas kernels, scatter_gradients(): pl.pallas_call(scatter_kernel, in_specs=[pl.BlockSpec(memory_space=pltpu....  28.5 us

profile of v5, /device:TPU:1, one launch (start us, length us, event | category | flops | bytes accessed | tf_op | source)
XLA Modules:
  0.0 112.1 jit_solution(9464925400233343741)
XLA Ops:
  1.3 0.0 copy-start
  1.3 0.0 copy-start.1
  1.3 0.0 copy-start.2
  1.3 33.4 %gather_features.1 = (bf16[128,128,128]{2,1,0:T(8,128)(2,1)S(1)}, bf16[32,128,256]{2,1,0:T(8,128)(2,1)S(1)}, f32[32,128]{1,0:T(8,128)S(1)}, f32[32,128]{1,0:T(8,...) custom-call(s32[1,1]{1,0:T(1,128)S(6)} %copy.11.count_ref, s32[1,128]{1,0:T(1,128)} %bitcast.6, ...), custom_call_target="tpu_custom_call" | custom-call | tf_op jit(solution)/shard_map/gather_features/pallas_call | solution.py:399
  34.7 0.0 copy-done
  34.7 0.0 copy-done.1
  34.8 0.0 copy-done.2
  34.8 48.1 %dense_layer.1 = (f32[256,128]{1,0:T(8,128)S(1)}, bf16[32,128,256]{2,1,0:T(8,128)(2,1)S(1)}, f32[16,128]{1,0:T(8,128)S(1)}) custom-call(s32[1,1]{1,0:T(1,128)S(6)} %copy.11.count_ref, s32[5,128]{1,0:T(8,128)S(1)} %get-tuple-element.20.info_ref, bf16[128,128,128]{2,1,0:T(8,128)(2,1)S(1)} %get-tuple-element.21.tiles_ref, ...), custom_call_target="tpu_custom_call" | custom-call | tf_op jit(solution)/shard_map/dense_layer/pallas_call | solution.py:708
  82.8 28.5 %scatter_gradients.1 = (f32[256,128]{1,0:T(8,128)S(1)}, f32[128,128]{1,0:T(8,128)S(1)}, f32[1,128]{1,0:T(1,128)S(1)}) custom-call(s32[1,1]{1,0:T(1,128)S(6)} %copy.11.count_ref, s32[5,128]{1,0:T(8,128)S(1)} %get-tuple-element.25.info_ref, bf16[128,128,128]{2,1,0:T(8,128)(2,1)S(1)} %get-tuple-element.21.tiles_ref, ...), custom_call_target="tpu_custom_call" | custom-call | tf_op jit(solution)/shard_map/scatter_gradients/pallas_call | solution.py:910
  111.3 0.8 put_out.1
Async XLA Ops:
  1.3 33.5 %copy-start = (f32[256,128]{1,0:T(8,128)S(1)}, f32[256,128]{1,0:T(8,128)}, u32[]{:S(2)}) copy-start(f32[256,128]{1,0:T(8,128)} %grad_ref.1) | copy-start | bytes 393220
  1.3 33.5 %copy-start.1 = (f32[128,128]{1,0:T(8,128)S(1)}, f32[128,128]{1,0:T(8,128)}, u32[]{:S(2)}) copy-start(f32[128,128]{1,0:T(8,128)} %w_ref.1) | copy-start | bytes 196612
  1.3 33.5 %copy-start.2 = (f32[128]{0:T(128)S(1)}, f32[128]{0:T(128)}, u32[]{:S(2)}) copy-start(f32[128]{0:T(128)} %param.9) | copy-start | bytes 1540
